TPU v7x, 1024 devices: a whole 4x8x16 slice. The times are simulated.
1024 devices in a mesh: dp: 64 (over y, x, core), section: 16 (over z).
Axes of the slice: x: 4, y: 8, z: 16, core: 2. Of those that a mesh axis runs over, the one named last changes fastest.
Arguments:
- inputs: bfloat16 [8192, 3072], P('dp'), may hold values from -6 to 6
- tiles: bfloat16 [16, 72, 128, 128], P('section'), may hold values from -0.3125 to 0.3125
- tile_rows: int32 [16, 72], P('section'), may hold values from 0 to 23, as said below
- out_grad: bfloat16 [8192, 3072], P('dp'), may hold values from -0.119628906 to 0.119628906
Outputs:
- weight_grad: float32 [128, 16, 72, 128], P('dp', 'section')
Inputs may be any that keep to these rules, and one draw needn't show every extreme that they name: `tile_rows`: in each layer, the 3 entries of every aligned group of 3 consecutive tiles (one tile column) name different tile rows.
All inputs are finite; a program needn't handle non-finite values.
Results may differ from a plain program's by a relative error of at most 0.025.
Values may be sent and summed in bfloat16 or wider, within the bound.
A program may use at most 32 MiB of HBM per device.

v0:
```python
import jax
import jax.numpy as jnp
from jax import lax
from jax.sharding import PartitionSpec as P

NMB = 4


EPS = 1e-06


def from_behind(array, axis, by):
    peers = lax.axis_size(axis)
    pairs = [(i, i + by) for i in range(peers) if 0 <= i + by < peers]
    return lax.ppermute(array, axis, pairs)


def row_scale(h):
    hf = h.astype(jnp.float32)
    return (hf, lax.rsqrt(jnp.mean(hf * hf, axis=1, keepdims=True) + EPS))


def layer_forward(h, tile_set, rows, nb, kpc):
    count = h.shape[0]
    blk = tile_set.shape[-1]
    hf, scale = row_scale(h)
    low = (hf * scale).astype(jnp.bfloat16)
    picked = jnp.take(low.reshape(count, nb, blk), rows, axis=1).reshape(count, nb, kpc, blk)
    mixed = jnp.einsum(
        "mnkr,nkrc->mnc",
        picked,
        tile_set.reshape(nb, kpc, blk, blk),
        preferred_element_type=jnp.float32,
    ).reshape(count, nb * blk)
    act = jnp.tanh(mixed)
    out = (hf + act).astype(jnp.bfloat16)
    return (out, act)


def layer_backward(h, act, grad, tile_set, rows, nb, kpc):
    count = h.shape[0]
    blk = tile_set.shape[-1]
    hf, scale = row_scale(h)
    gradf = grad.astype(jnp.float32)
    dz = (gradf * (1.0 - act * act)).astype(jnp.bfloat16)
    back = jnp.einsum(
        "mnc,nkrc->mnkr",
        dz.reshape(count, nb, blk),
        tile_set.reshape(nb, kpc, blk, blk),
        preferred_element_type=jnp.float32,
    )
    onehot = (rows[:, None] == jnp.arange(nb, dtype=jnp.int32)[None, :]).astype(jnp.float32)
    spread = jnp.einsum(
        "mtr,tb->mbr", back.reshape(count, nb * kpc, blk), onehot, precision=lax.Precision.HIGHEST
    ).reshape(count, nb * blk)
    normed = hf * scale
    inner = jnp.mean(spread * normed, axis=1, keepdims=True)
    result = gradf + scale * (spread - normed * inner)
    return (dz, result.astype(jnp.bfloat16))


def local(inputs, tiles, tile_rows, out_grad):
    sections = lax.axis_size("section")
    section = lax.axis_index("section")
    tile_set = tiles[0]
    rows = tile_rows[0]
    blk = tiles.shape[-1]
    width = inputs.shape[1]
    nb = width // blk
    kpc = tiles.shape[1] // nb
    total = inputs.shape[0]
    groups = NMB
    group_rows = total // groups
    feed = inputs.reshape(groups, group_rows, width)
    seeds = out_grad.reshape(groups, group_rows, width)
    saved_h = jnp.zeros((groups, group_rows, width), jnp.bfloat16)
    saved_act = jnp.zeros((groups, group_rows, width), jnp.float32)
    blank = jnp.zeros((group_rows, width), jnp.bfloat16)

    def forward_step(step, carry):
        incoming, keep_h, keep_act = carry
        slot = step - section
        live = jnp.logical_and(slot >= 0, slot < groups)
        index = jnp.clip(slot, 0, groups - 1)
        start_h = jnp.where(section == 0, feed[index], incoming)

        def forward_work(state):
            store_h, store_act = state
            out, act = layer_forward(start_h, tile_set, rows, nb, kpc)
            store_h = lax.dynamic_update_index_in_dim(store_h, start_h, index, 0)
            store_act = lax.dynamic_update_index_in_dim(store_act, act, index, 0)
            return (out, store_h, store_act)

        def forward_skip(state):
            return (blank,) + state

        out, keep_h, keep_act = lax.cond(live, forward_work, forward_skip, (keep_h, keep_act))
        incoming = from_behind(out, "section", 1)
        return (incoming, keep_h, keep_act)

    unused, saved_h, saved_act = lax.fori_loop(
        0, sections + groups - 1, forward_step, (blank, saved_h, saved_act)
    )
    saved_dz = jnp.zeros((groups, group_rows, width), jnp.bfloat16)

    def backward_step(step, carry):
        incoming, keep_dz = carry
        slot = step - (sections - 1 - section)
        live = jnp.logical_and(slot >= 0, slot < groups)
        index = jnp.clip(slot, 0, groups - 1)
        grad_in = jnp.where(section == sections - 1, seeds[index], incoming)

        def backward_work(store_dz):
            dz, current = layer_backward(
                saved_h[index], saved_act[index], grad_in, tile_set, rows, nb, kpc
            )
            store_dz = lax.dynamic_update_index_in_dim(store_dz, dz, index, 0)
            return (current, store_dz)

        def backward_skip(store_dz):
            return (blank, store_dz)

        out, keep_dz = lax.cond(live, backward_work, backward_skip, keep_dz)
        incoming = from_behind(out, "section", -1)
        return (incoming, keep_dz)

    unused, saved_dz = lax.fori_loop(0, sections + groups - 1, backward_step, (blank, saved_dz))
    flat_h = saved_h.reshape(total, width)
    hf, scale = row_scale(flat_h)
    low = (hf * scale).astype(jnp.bfloat16)
    picked = jnp.take(low.reshape(total, nb, blk), rows, axis=1).reshape(total, nb, kpc, blk)
    dz_all = saved_dz.reshape(total, nb, blk)
    term = jnp.einsum("mnkr,mnc->rnkc", picked, dz_all, preferred_element_type=jnp.float32)
    term = term.reshape(blk, 1, nb * kpc, blk)
    return lax.psum_scatter(term, "dp", scatter_dimension=0, tiled=True)


def solution(mesh):
    return jax.shard_map(
        local,
        mesh=mesh,
        in_specs=(P("dp", None), P("section", None, None, None), P("section", None), P("dp", None)),
        out_specs=P("dp", "section", None, None),
        check_vma=False,
    )
```

profile of v0, /device:TPU:6, one launch (start us, length us, event | category | flops | bytes accessed | tf_op | source)
XLA Modules:
  0.0 725.1 jit_solution(1519847254613893839)
XLA Ops:
  11.7 207.2 %while.38 = (s32[]{:T(128)}, bf16[32,3072]{1,0:T(8,128)(2,1)S(1)}, bf16[4,32,3072]{2,1,0:T(8,128)(2,1)}, f32[4,32,3072]{2,1,0:T(8,128)}, s32[]{:T(128)}, /*index...) while((s32[]{:T(128)}, bf16[32,3072]{1,0:T(8,128)(2,1)S(1)}, ...), condition=%wide.region_4.5_spmd, body=%wide.region_0.4_spmd.sunk | while | flops 76777136 | bytes 9837579 | solution.py:101
  62.7 8.8 %collective-permute-start = (bf16[32,3072]{1,0:T(8,128)(2,1)}, bf16[32,3072]{1,0:T(8,128)(2,1)S(1)}, u32[]{:S(2)}, u32[]{:S(2)}) collective-permute-start(bf16[32,3072]{1,0:T(8,128)(2,1)} %get-tuple-element.762), channel_id=1, source_target_pairs={{0,1},{1,2},{2,3},{3,4},{4,5},{5,6},{6,7},{7,8},{8,9},{9,10},{10,1... | collective-permute-start | bytes 589832 | tf_op jit(solution)/shard_map/while/body/eval_jaxpr/ppermute | solution.py:15
  124.3 13.5 %collective-permute-start = (bf16[32,3072]{1,0:T(8,128)(2,1)}, bf16[32,3072]{1,0:T(8,128)(2,1)S(1)}, u32[]{:S(2)}, u32[]{:S(2)}) collective-permute-start(bf16[32,3072]{1,0:T(8,128)(2,1)} %get-tuple-element.762), channel_id=1, source_target_pairs={{0,1},{1,2},{2,3},{3,4},{4,5},{5,6},{6,7},{7,8},{8,9},{9,10},{10,1... | collective-permute-start | bytes 589832 | tf_op jit(solution)/shard_map/while/body/eval_jaxpr/ppermute | solution.py:15
  221.4 312.3 %while.39 = (s32[]{:T(128)}, bf16[32,3072]{1,0:T(8,128)(2,1)S(1)}, bf16[4,32,3072]{2,1,0:T(8,128)(2,1)}, s32[]{:T(128)}, pred[]{:T(512)}, /*index=5*/bf16[4,32,3...) while((s32[]{:T(128)}, bf16[32,3072]{1,0:T(8,128)(2,1)S(1)}, ...), condition=%wide.region_10.11_spmd, body=%wide.region_5.10_spmd.sunk | while | flops 162596576 | bytes 10815724 | solution.py:127
  222.8 8.5 %collective-permute-done.1 = bf16[32,3072]{1,0:T(8,128)(2,1)S(1)} collective-permute-done((bf16[32,3072]{1,0:T(8,128)(2,1)S(1)}, bf16[32,3072]{1,0:T(8,128)(2,1)S(1)}, u32[]{:S(2)}, u32[]{:S(2)}) %collective-permute-start.1) | collective-permute-done | bytes 196640 | tf_op jit(solution)/shard_map/while/body/eval_jaxpr/ppermute | solution.py:15
  232.6 7.5 %collective-permute-done.1 = bf16[32,3072]{1,0:T(8,128)(2,1)S(1)} collective-permute-done((bf16[32,3072]{1,0:T(8,128)(2,1)S(1)}, bf16[32,3072]{1,0:T(8,128)(2,1)S(1)}, u32[]{:S(2)}, u32[]{:S(2)}) %collective-permute-start.1) | collective-permute-done | bytes 196640 | tf_op jit(solution)/shard_map/while/body/eval_jaxpr/ppermute | solution.py:15
  241.4 7.8 %collective-permute-done.1 = bf16[32,3072]{1,0:T(8,128)(2,1)S(1)} collective-permute-done((bf16[32,3072]{1,0:T(8,128)(2,1)S(1)}, bf16[32,3072]{1,0:T(8,128)(2,1)S(1)}, u32[]{:S(2)}, u32[]{:S(2)}) %collective-permute-start.1) | collective-permute-done | bytes 196640 | tf_op jit(solution)/shard_map/while/body/eval_jaxpr/ppermute | solution.py:15
  250.6 7.8 %collective-permute-done.1 = bf16[32,3072]{1,0:T(8,128)(2,1)S(1)} collective-permute-done((bf16[32,3072]{1,0:T(8,128)(2,1)S(1)}, bf16[32,3072]{1,0:T(8,128)(2,1)S(1)}, u32[]{:S(2)}, u32[]{:S(2)}) %collective-permute-start.1) | collective-permute-done | bytes 196640 | tf_op jit(solution)/shard_map/while/body/eval_jaxpr/ppermute | solution.py:15
  259.7 9.2 %collective-permute-done.1 = bf16[32,3072]{1,0:T(8,128)(2,1)S(1)} collective-permute-done((bf16[32,3072]{1,0:T(8,128)(2,1)S(1)}, bf16[32,3072]{1,0:T(8,128)(2,1)S(1)}, u32[]{:S(2)}, u32[]{:S(2)}) %collective-permute-start.1) | collective-permute-done | bytes 196640 | tf_op jit(solution)/shard_map/while/body/eval_jaxpr/ppermute | solution.py:15
  270.3 10.9 %collective-permute-done.1 = bf16[32,3072]{1,0:T(8,128)(2,1)S(1)} collective-permute-done((bf16[32,3072]{1,0:T(8,128)(2,1)S(1)}, bf16[32,3072]{1,0:T(8,128)(2,1)S(1)}, u32[]{:S(2)}, u32[]{:S(2)}) %collective-permute-start.1) | collective-permute-done | bytes 196640 | tf_op jit(solution)/shard_map/while/body/eval_jaxpr/ppermute | solution.py:15
  282.5 8.8 %collective-permute-done.1 = bf16[32,3072]{1,0:T(8,128)(2,1)S(1)} collective-permute-done((bf16[32,3072]{1,0:T(8,128)(2,1)S(1)}, bf16[32,3072]{1,0:T(8,128)(2,1)S(1)}, u32[]{:S(2)}, u32[]{:S(2)}) %collective-permute-start.1) | collective-permute-done | bytes 196640 | tf_op jit(solution)/shard_map/while/body/eval_jaxpr/ppermute | solution.py:15
  292.6 9.4 %collective-permute-done.1 = bf16[32,3072]{1,0:T(8,128)(2,1)S(1)} collective-permute-done((bf16[32,3072]{1,0:T(8,128)(2,1)S(1)}, bf16[32,3072]{1,0:T(8,128)(2,1)S(1)}, u32[]{:S(2)}, u32[]{:S(2)}) %collective-permute-start.1) | collective-permute-done | bytes 196640 | tf_op jit(solution)/shard_map/while/body/eval_jaxpr/ppermute | solution.py:15
  303.4 7.7 %collective-permute-done.1 = bf16[32,3072]{1,0:T(8,128)(2,1)S(1)} collective-permute-done((bf16[32,3072]{1,0:T(8,128)(2,1)S(1)}, bf16[32,3072]{1,0:T(8,128)(2,1)S(1)}, u32[]{:S(2)}, u32[]{:S(2)}) %collective-permute-start.1) | collective-permute-done | bytes 196640 | tf_op jit(solution)/shard_map/while/body/eval_jaxpr/ppermute | solution.py:15
  312.4 7.9 %collective-permute-done.1 = bf16[32,3072]{1,0:T(8,128)(2,1)S(1)} collective-permute-done((bf16[32,3072]{1,0:T(8,128)(2,1)S(1)}, bf16[32,3072]{1,0:T(8,128)(2,1)S(1)}, u32[]{:S(2)}, u32[]{:S(2)}) %collective-permute-start.1) | collective-permute-done | bytes 196640 | tf_op jit(solution)/shard_map/while/body/eval_jaxpr/ppermute | solution.py:15
  329.2 7.6 %collective-permute-done.1 = bf16[32,3072]{1,0:T(8,128)(2,1)S(1)} collective-permute-done((bf16[32,3072]{1,0:T(8,128)(2,1)S(1)}, bf16[32,3072]{1,0:T(8,128)(2,1)S(1)}, u32[]{:S(2)}, u32[]{:S(2)}) %collective-permute-start.1) | collective-permute-done | bytes 196640 | tf_op jit(solution)/shard_map/while/body/eval_jaxpr/ppermute | solution.py:15
  338.2 7.5 %collective-permute-done.1 = bf16[32,3072]{1,0:T(8,128)(2,1)S(1)} collective-permute-done((bf16[32,3072]{1,0:T(8,128)(2,1)S(1)}, bf16[32,3072]{1,0:T(8,128)(2,1)S(1)}, u32[]{:S(2)}, u32[]{:S(2)}) %collective-permute-start.1) | collective-permute-done | bytes 196640 | tf_op jit(solution)/shard_map/while/body/eval_jaxpr/ppermute | solution.py:15
  347.0 7.5 %collective-permute-done.1 = bf16[32,3072]{1,0:T(8,128)(2,1)S(1)} collective-permute-done((bf16[32,3072]{1,0:T(8,128)(2,1)S(1)}, bf16[32,3072]{1,0:T(8,128)(2,1)S(1)}, u32[]{:S(2)}, u32[]{:S(2)}) %collective-permute-start.1) | collective-permute-done | bytes 196640 | tf_op jit(solution)/shard_map/while/body/eval_jaxpr/ppermute | solution.py:15
  355.8 112.6 %collective-permute-done.1 = bf16[32,3072]{1,0:T(8,128)(2,1)S(1)} collective-permute-done((bf16[32,3072]{1,0:T(8,128)(2,1)S(1)}, bf16[32,3072]{1,0:T(8,128)(2,1)S(1)}, u32[]{:S(2)}, u32[]{:S(2)}) %collective-permute-start.1) | collective-permute-done | bytes 196640 | tf_op jit(solution)/shard_map/while/body/eval_jaxpr/ppermute | solution.py:15
  468.4 7.4 %conditional.5 = (bf16[32,3072]{1,0:T(8,128)(2,1)S(1)}, bf16[4,32,3072]{2,1,0:T(8,128)(2,1)}) conditional(s32[]{:T(128)} %convert_element_type.141, bf16[4,32,3072]{2,1,0:T(8,128)(2,1)} %get-tuple-element.838, (pred[]{:T(512)}, s32[]{:T(128)}, bf16[4,32,3072]{2,1,0:T(8,128)(2,1)S(1)}, bf16[32,3072]{1,0:T(8,128)(2,1)S(1)}, ...), branch_computations={%region_6.6_spmd, %region_7.9_spmd} | conditional | flops 162596576 | bytes 10029017 | solution.py:123
  477.2 8.1 %collective-permute-done.1 = bf16[32,3072]{1,0:T(8,128)(2,1)S(1)} collective-permute-done((bf16[32,3072]{1,0:T(8,128)(2,1)S(1)}, bf16[32,3072]{1,0:T(8,128)(2,1)S(1)}, u32[]{:S(2)}, u32[]{:S(2)}) %collective-permute-start.1) | collective-permute-done | bytes 196640 | tf_op jit(solution)/shard_map/while/body/eval_jaxpr/ppermute | solution.py:15
  485.2 7.4 %conditional.5 = (bf16[32,3072]{1,0:T(8,128)(2,1)S(1)}, bf16[4,32,3072]{2,1,0:T(8,128)(2,1)}) conditional(s32[]{:T(128)} %convert_element_type.141, bf16[4,32,3072]{2,1,0:T(8,128)(2,1)} %get-tuple-element.838, (pred[]{:T(512)}, s32[]{:T(128)}, bf16[4,32,3072]{2,1,0:T(8,128)(2,1)S(1)}, bf16[32,3072]{1,0:T(8,128)(2,1)S(1)}, ...), branch_computations={%region_6.6_spmd, %region_7.9_spmd} | conditional | flops 162596576 | bytes 10029017 | solution.py:123
  494.0 9.0 %collective-permute-done.1 = bf16[32,3072]{1,0:T(8,128)(2,1)S(1)} collective-permute-done((bf16[32,3072]{1,0:T(8,128)(2,1)S(1)}, bf16[32,3072]{1,0:T(8,128)(2,1)S(1)}, u32[]{:S(2)}, u32[]{:S(2)}) %collective-permute-start.1) | collective-permute-done | bytes 196640 | tf_op jit(solution)/shard_map/while/body/eval_jaxpr/ppermute | solution.py:15
  518.7 7.5 %conditional.5 = (bf16[32,3072]{1,0:T(8,128)(2,1)S(1)}, bf16[4,32,3072]{2,1,0:T(8,128)(2,1)}) conditional(s32[]{:T(128)} %convert_element_type.141, bf16[4,32,3072]{2,1,0:T(8,128)(2,1)} %get-tuple-element.838, (pred[]{:T(512)}, s32[]{:T(128)}, bf16[4,32,3072]{2,1,0:T(8,128)(2,1)S(1)}, bf16[32,3072]{1,0:T(8,128)(2,1)S(1)}, ...), branch_computations={%region_6.6_spmd, %region_7.9_spmd} | conditional | flops 162596576 | bytes 10029017 | solution.py:123
  550.0 168.2 %reduce-scatter.4.cloned.1.call-done = f32[2,1,72,128]{3,2,1,0:T(8,128)} async-done(((f32[128,1,72,128]{3,2,1,0:T(8,128)}), f32[2,1,72,128]{3,2,1,0:T(8,128)}) %reduce-scatter.4.cloned.1.call-update) | async-done | bytes 73744
  (247 shorter events, 321.0 us)
Async XLA Ops:
  6.5 711.7 %reduce-scatter.4.cloned.1.call-start = ((), (), s32[]{:S(2)}) async-start(), calls=%async_computation.1 | async-start | bytes 4792320
  62.7 12.3 %collective-permute-start = (bf16[32,3072]{1,0:T(8,128)(2,1)}, bf16[32,3072]{1,0:T(8,128)(2,1)S(1)}, u32[]{:S(2)}, u32[]{:S(2)}) collective-permute-start(bf16[32,3072]{1,0:T(8,128)(2,1)} %get-tuple-element.762), channel_id=1, source_target_pairs={{0,1},{1,2},{2,3},{3,4},{4,5},{5,6},{6,7},{7,8},{8,9},{9,10},{10,1... | collective-permute-start | bytes 589832 | tf_op jit(solution)/shard_map/while/body/eval_jaxpr/ppermute | solution.py:15
  84.1 12.1 %collective-permute-start = (bf16[32,3072]{1,0:T(8,128)(2,1)}, bf16[32,3072]{1,0:T(8,128)(2,1)S(1)}, u32[]{:S(2)}, u32[]{:S(2)}) collective-permute-start(bf16[32,3072]{1,0:T(8,128)(2,1)} %get-tuple-element.762), channel_id=1, source_target_pairs={{0,1},{1,2},{2,3},{3,4},{4,5},{5,6},{6,7},{7,8},{8,9},{9,10},{10,1... | collective-permute-start | bytes 589832 | tf_op jit(solution)/shard_map/while/body/eval_jaxpr/ppermute | solution.py:15
  106.0 9.1 %collective-permute-start = (bf16[32,3072]{1,0:T(8,128)(2,1)}, bf16[32,3072]{1,0:T(8,128)(2,1)S(1)}, u32[]{:S(2)}, u32[]{:S(2)}) collective-permute-start(bf16[32,3072]{1,0:T(8,128)(2,1)} %get-tuple-element.762), channel_id=1, source_target_pairs={{0,1},{1,2},{2,3},{3,4},{4,5},{5,6},{6,7},{7,8},{8,9},{9,10},{10,1... | collective-permute-start | bytes 589832 | tf_op jit(solution)/shard_map/while/body/eval_jaxpr/ppermute | solution.py:15
  124.3 17.8 %collective-permute-start = (bf16[32,3072]{1,0:T(8,128)(2,1)}, bf16[32,3072]{1,0:T(8,128)(2,1)S(1)}, u32[]{:S(2)}, u32[]{:S(2)}) collective-permute-start(bf16[32,3072]{1,0:T(8,128)(2,1)} %get-tuple-element.762), channel_id=1, source_target_pairs={{0,1},{1,2},{2,3},{3,4},{4,5},{5,6},{6,7},{7,8},{8,9},{9,10},{10,1... | collective-permute-start | bytes 589832 | tf_op jit(solution)/shard_map/while/body/eval_jaxpr/ppermute | solution.py:15
  161.4 9.0 %collective-permute-start = (bf16[32,3072]{1,0:T(8,128)(2,1)}, bf16[32,3072]{1,0:T(8,128)(2,1)S(1)}, u32[]{:S(2)}, u32[]{:S(2)}) collective-permute-start(bf16[32,3072]{1,0:T(8,128)(2,1)} %get-tuple-element.762), channel_id=1, source_target_pairs={{0,1},{1,2},{2,3},{3,4},{4,5},{5,6},{6,7},{7,8},{8,9},{9,10},{10,1... | collective-permute-start | bytes 589832 | tf_op jit(solution)/shard_map/while/body/eval_jaxpr/ppermute | solution.py:15
  171.1 9.0 %collective-permute-start = (bf16[32,3072]{1,0:T(8,128)(2,1)}, bf16[32,3072]{1,0:T(8,128)(2,1)S(1)}, u32[]{:S(2)}, u32[]{:S(2)}) collective-permute-start(bf16[32,3072]{1,0:T(8,128)(2,1)} %get-tuple-element.762), channel_id=1, source_target_pairs={{0,1},{1,2},{2,3},{3,4},{4,5},{5,6},{6,7},{7,8},{8,9},{9,10},{10,1... | collective-permute-start | bytes 589832 | tf_op jit(solution)/shard_map/while/body/eval_jaxpr/ppermute | solution.py:15
  180.7 9.0 %collective-permute-start = (bf16[32,3072]{1,0:T(8,128)(2,1)}, bf16[32,3072]{1,0:T(8,128)(2,1)S(1)}, u32[]{:S(2)}, u32[]{:S(2)}) collective-permute-start(bf16[32,3072]{1,0:T(8,128)(2,1)} %get-tuple-element.762), channel_id=1, source_target_pairs={{0,1},{1,2},{2,3},{3,4},{4,5},{5,6},{6,7},{7,8},{8,9},{9,10},{10,1... | collective-permute-start | bytes 589832 | tf_op jit(solution)/shard_map/while/body/eval_jaxpr/ppermute | solution.py:15
  190.4 9.0 %collective-permute-start = (bf16[32,3072]{1,0:T(8,128)(2,1)}, bf16[32,3072]{1,0:T(8,128)(2,1)S(1)}, u32[]{:S(2)}, u32[]{:S(2)}) collective-permute-start(bf16[32,3072]{1,0:T(8,128)(2,1)} %get-tuple-element.762), channel_id=1, source_target_pairs={{0,1},{1,2},{2,3},{3,4},{4,5},{5,6},{6,7},{7,8},{8,9},{9,10},{10,1... | collective-permute-start | bytes 589832 | tf_op jit(solution)/shard_map/while/body/eval_jaxpr/ppermute | solution.py:15
  200.0 9.0 %collective-permute-start = (bf16[32,3072]{1,0:T(8,128)(2,1)}, bf16[32,3072]{1,0:T(8,128)(2,1)S(1)}, u32[]{:S(2)}, u32[]{:S(2)}) collective-permute-start(bf16[32,3072]{1,0:T(8,128)(2,1)} %get-tuple-element.762), channel_id=1, source_target_pairs={{0,1},{1,2},{2,3},{3,4},{4,5},{5,6},{6,7},{7,8},{8,9},{9,10},{10,1... | collective-permute-start | bytes 589832 | tf_op jit(solution)/shard_map/while/body/eval_jaxpr/ppermute | solution.py:15
  209.7 9.3 %collective-permute-start = (bf16[32,3072]{1,0:T(8,128)(2,1)}, bf16[32,3072]{1,0:T(8,128)(2,1)S(1)}, u32[]{:S(2)}, u32[]{:S(2)}) collective-permute-start(bf16[32,3072]{1,0:T(8,128)(2,1)} %get-tuple-element.762), channel_id=1, source_target_pairs={{0,1},{1,2},{2,3},{3,4},{4,5},{5,6},{6,7},{7,8},{8,9},{9,10},{10,1... | collective-permute-start | bytes 589832 | tf_op jit(solution)/shard_map/while/body/eval_jaxpr/ppermute | solution.py:15
  221.5 9.8 %collective-permute-start.1 = (bf16[32,3072]{1,0:T(8,128)(2,1)S(1)}, bf16[32,3072]{1,0:T(8,128)(2,1)S(1)}, u32[]{:S(2)}, u32[]{:S(2)}) collective-permute-start(bf16[32,3072]{1,0:T(8,128)(2,1)S(1)} %get-tuple-element.775), channel_id=1, source_target_pairs={{1,0},{2,1},{3,2},{4,3},{5,4},{6,5},{7,6},{8,7},{9,8},{10,9},{11,1... | collective-permute-start | bytes 589832 | tf_op jit(solution)/shard_map/while/body/eval_jaxpr/ppermute | solution.py:15
  240.1 9.1 %collective-permute-start.1 = (bf16[32,3072]{1,0:T(8,128)(2,1)S(1)}, bf16[32,3072]{1,0:T(8,128)(2,1)S(1)}, u32[]{:S(2)}, u32[]{:S(2)}) collective-permute-start(bf16[32,3072]{1,0:T(8,128)(2,1)S(1)} %get-tuple-element.775), channel_id=1, source_target_pairs={{1,0},{2,1},{3,2},{4,3},{5,4},{6,5},{7,6},{8,7},{9,8},{10,9},{11,1... | collective-permute-start | bytes 589832 | tf_op jit(solution)/shard_map/while/body/eval_jaxpr/ppermute | solution.py:15
  249.3 9.1 %collective-permute-start.1 = (bf16[32,3072]{1,0:T(8,128)(2,1)S(1)}, bf16[32,3072]{1,0:T(8,128)(2,1)S(1)}, u32[]{:S(2)}, u32[]{:S(2)}) collective-permute-start(bf16[32,3072]{1,0:T(8,128)(2,1)S(1)} %get-tuple-element.775), channel_id=1, source_target_pairs={{1,0},{2,1},{3,2},{4,3},{5,4},{6,5},{7,6},{8,7},{9,8},{10,9},{11,1... | collective-permute-start | bytes 589832 | tf_op jit(solution)/shard_map/while/body/eval_jaxpr/ppermute | solution.py:15
  258.4 10.5 %collective-permute-start.1 = (bf16[32,3072]{1,0:T(8,128)(2,1)S(1)}, bf16[32,3072]{1,0:T(8,128)(2,1)S(1)}, u32[]{:S(2)}, u32[]{:S(2)}) collective-permute-start(bf16[32,3072]{1,0:T(8,128)(2,1)S(1)} %get-tuple-element.775), channel_id=1, source_target_pairs={{1,0},{2,1},{3,2},{4,3},{5,4},{6,5},{7,6},{8,7},{9,8},{10,9},{11,1... | collective-permute-start | bytes 589832 | tf_op jit(solution)/shard_map/while/body/eval_jaxpr/ppermute | solution.py:15
  269.0 12.2 %collective-permute-start.1 = (bf16[32,3072]{1,0:T(8,128)(2,1)S(1)}, bf16[32,3072]{1,0:T(8,128)(2,1)S(1)}, u32[]{:S(2)}, u32[]{:S(2)}) collective-permute-start(bf16[32,3072]{1,0:T(8,128)(2,1)S(1)} %get-tuple-element.775), channel_id=1, source_target_pairs={{1,0},{2,1},{3,2},{4,3},{5,4},{6,5},{7,6},{8,7},{9,8},{10,9},{11,1... | collective-permute-start | bytes 589832 | tf_op jit(solution)/shard_map/while/body/eval_jaxpr/ppermute | solution.py:15
  281.2 10.1 %collective-permute-start.1 = (bf16[32,3072]{1,0:T(8,128)(2,1)S(1)}, bf16[32,3072]{1,0:T(8,128)(2,1)S(1)}, u32[]{:S(2)}, u32[]{:S(2)}) collective-permute-start(bf16[32,3072]{1,0:T(8,128)(2,1)S(1)} %get-tuple-element.775), channel_id=1, source_target_pairs={{1,0},{2,1},{3,2},{4,3},{5,4},{6,5},{7,6},{8,7},{9,8},{10,9},{11,1... | collective-permute-start | bytes 589832 | tf_op jit(solution)/shard_map/while/body/eval_jaxpr/ppermute | solution.py:15
  291.3 10.7 %collective-permute-start.1 = (bf16[32,3072]{1,0:T(8,128)(2,1)S(1)}, bf16[32,3072]{1,0:T(8,128)(2,1)S(1)}, u32[]{:S(2)}, u32[]{:S(2)}) collective-permute-start(bf16[32,3072]{1,0:T(8,128)(2,1)S(1)} %get-tuple-element.775), channel_id=1, source_target_pairs={{1,0},{2,1},{3,2},{4,3},{5,4},{6,5},{7,6},{8,7},{9,8},{10,9},{11,1... | collective-permute-start | bytes 589832 | tf_op jit(solution)/shard_map/while/body/eval_jaxpr/ppermute | solution.py:15
  302.1 9.0 %collective-permute-start.1 = (bf16[32,3072]{1,0:T(8,128)(2,1)S(1)}, bf16[32,3072]{1,0:T(8,128)(2,1)S(1)}, u32[]{:S(2)}, u32[]{:S(2)}) collective-permute-start(bf16[32,3072]{1,0:T(8,128)(2,1)S(1)} %get-tuple-element.775), channel_id=1, source_target_pairs={{1,0},{2,1},{3,2},{4,3},{5,4},{6,5},{7,6},{8,7},{9,8},{10,9},{11,1... | collective-permute-start | bytes 589832 | tf_op jit(solution)/shard_map/while/body/eval_jaxpr/ppermute | solution.py:15
  311.1 9.2 %collective-permute-start.1 = (bf16[32,3072]{1,0:T(8,128)(2,1)S(1)}, bf16[32,3072]{1,0:T(8,128)(2,1)S(1)}, u32[]{:S(2)}, u32[]{:S(2)}) collective-permute-start(bf16[32,3072]{1,0:T(8,128)(2,1)S(1)} %get-tuple-element.775), channel_id=1, source_target_pairs={{1,0},{2,1},{3,2},{4,3},{5,4},{6,5},{7,6},{8,7},{9,8},{10,9},{11,1... | collective-permute-start | bytes 589832 | tf_op jit(solution)/shard_map/while/body/eval_jaxpr/ppermute | solution.py:15
  327.9 8.9 %collective-permute-start.1 = (bf16[32,3072]{1,0:T(8,128)(2,1)S(1)}, bf16[32,3072]{1,0:T(8,128)(2,1)S(1)}, u32[]{:S(2)}, u32[]{:S(2)}) collective-permute-start(bf16[32,3072]{1,0:T(8,128)(2,1)S(1)} %get-tuple-element.775), channel_id=1, source_target_pairs={{1,0},{2,1},{3,2},{4,3},{5,4},{6,5},{7,6},{8,7},{9,8},{10,9},{11,1... | collective-permute-start | bytes 589832 | tf_op jit(solution)/shard_map/while/body/eval_jaxpr/ppermute | solution.py:15
  354.5 113.9 %collective-permute-start.1 = (bf16[32,3072]{1,0:T(8,128)(2,1)S(1)}, bf16[32,3072]{1,0:T(8,128)(2,1)S(1)}, u32[]{:S(2)}, u32[]{:S(2)}) collective-permute-start(bf16[32,3072]{1,0:T(8,128)(2,1)S(1)} %get-tuple-element.775), channel_id=1, source_target_pairs={{1,0},{2,1},{3,2},{4,3},{5,4},{6,5},{7,6},{8,7},{9,8},{10,9},{11,1... | collective-permute-start | bytes 589832 | tf_op jit(solution)/shard_map/while/body/eval_jaxpr/ppermute | solution.py:15
  475.9 9.4 %collective-permute-start.1 = (bf16[32,3072]{1,0:T(8,128)(2,1)S(1)}, bf16[32,3072]{1,0:T(8,128)(2,1)S(1)}, u32[]{:S(2)}, u32[]{:S(2)}) collective-permute-start(bf16[32,3072]{1,0:T(8,128)(2,1)S(1)} %get-tuple-element.775), channel_id=1, source_target_pairs={{1,0},{2,1},{3,2},{4,3},{5,4},{6,5},{7,6},{8,7},{9,8},{10,9},{11,1... | collective-permute-start | bytes 589832 | tf_op jit(solution)/shard_map/while/body/eval_jaxpr/ppermute | solution.py:15
  492.7 10.3 %collective-permute-start.1 = (bf16[32,3072]{1,0:T(8,128)(2,1)S(1)}, bf16[32,3072]{1,0:T(8,128)(2,1)S(1)}, u32[]{:S(2)}, u32[]{:S(2)}) collective-permute-start(bf16[32,3072]{1,0:T(8,128)(2,1)S(1)} %get-tuple-element.775), channel_id=1, source_target_pairs={{1,0},{2,1},{3,2},{4,3},{5,4},{6,5},{7,6},{8,7},{9,8},{10,9},{11,1... | collective-permute-start | bytes 589832 | tf_op jit(solution)/shard_map/while/body/eval_jaxpr/ppermute | solution.py:15
  (18 other events, 133.7 us)
Sparse Core Ops, SparseCore 0:
  550.1 168.0 reduce-scatter.3
where the time goes:
time: 728 us; the launch traced here: 725 us
  waiting for transfers between devices  497 us (68%)
  starting transfers between devices  129 us (18%)
  other arithmetic  34.5 us (5%)
  local copies, waits for them, and re-layouts  33.4 us (5%)
  matrix products  16.5 us (2%)
  between operations  13.5 us (2%)
    ppermute x38, waiting for transfers between devices, from_behind(): return lax.ppermute(array, axis, pairs)  329 us
    unnamed x2, waiting for transfers between devices  168 us
    ppermute x38, starting transfers between devices, from_behind(): return lax.ppermute(array, axis, pairs)  129 us
  transfers between devices with their start and end apart: 39, of which 39 were waited for; matrix products, arithmetic and copies ran while one was open for 0% of the time, Pallas kernels for 0%

commit v1 on v0

v1 whole, which is shorter than its diff:
```python
import functools

import jax
import jax.numpy as jnp
from jax import lax
from jax.experimental import pallas as pl
from jax.experimental.pallas import tpu as pltpu
from jax.sharding import PartitionSpec as P

EPS = 1e-06
MB = 8
CHUNKS = 2
GRID_X = 4
GRID_Y = 8
GROUPS = 3
MESH = pl.DeviceIdType.MESH
F32 = jnp.float32
BF16 = jnp.bfloat16


def relay_kernel(sections, nmb, nb, rows_ref, perm_ref, last_ref, keep_ref, full_ref, x_ref, t_ref, og_ref,
                 u_ref, dz_ref,
                 hbuf, gbuf, fout, gout, hw, act, scl, prod, pref,
                 fsend, frecv, bsend, brecv):
    sec = lax.axis_index("section")
    width = nb * 128
    per = nb // CHUNKS
    first = sec == 0
    final = sec == sections - 1
    up = jnp.minimum(sec + 1, sections - 1)
    down = jnp.maximum(sec - 1, 0)

    barrier = pltpu.get_barrier_semaphore()

    @pl.when(sec > 0)
    def _():
        pl.semaphore_signal(barrier, inc=1, device_id={"section": down}, device_id_type=MESH)

    @pl.when(sec < sections - 1)
    def _():
        pl.semaphore_signal(barrier, inc=1, device_id={"section": up}, device_id_type=MESH)

    near = jnp.where(first, 0, 1) + jnp.where(final, 0, 1)
    pl.semaphore_wait(barrier, near)

    def fcopy(k, j):
        return pltpu.make_async_remote_copy(
            src_ref=fout.at[k, pl.ds(j * per, per)],
            dst_ref=hbuf.at[k, pl.ds(j * per, per)],
            send_sem=fsend.at[k],
            recv_sem=frecv.at[k],
            device_id={"section": up},
            device_id_type=MESH,
        )

    def bcopy(k, j):
        return pltpu.make_async_remote_copy(
            src_ref=gout.at[k, pl.ds(j * per, per)],
            dst_ref=gbuf.at[k, pl.ds(j * per, per)],
            send_sem=bsend.at[k],
            recv_sem=brecv.at[k],
            device_id={"section": down},
            device_id_type=MESH,
        )

    def fwhole(k):
        return pltpu.make_async_remote_copy(
            src_ref=fout.at[k], dst_ref=hbuf.at[k], send_sem=fsend.at[k], recv_sem=frecv.at[k],
            device_id={"section": up}, device_id_type=MESH,
        )

    def bwhole(k):
        return pltpu.make_async_remote_copy(
            src_ref=gout.at[k], dst_ref=gbuf.at[k], send_sem=bsend.at[k], recv_sem=brecv.at[k],
            device_id={"section": down}, device_id_type=MESH,
        )

    def forward(k, carry):
        @pl.when(first)
        def _():
            hbuf[k] = x_ref[k]

        @pl.when(sec > 0)
        def _():
            fwhole(k).wait_recv()

        total = jnp.zeros((MB, 128), F32)
        for b in range(nb):
            h = hbuf[k, b]
            hf = h.astype(F32)
            total = total + hf * hf
            hw[b] = h
        mean = jnp.sum(total, axis=1, keepdims=True) * (1.0 / width)
        scale = jnp.broadcast_to(lax.rsqrt(mean + EPS), (MB, 128))
        scl[k] = scale
        for c in range(nb):
            left = jnp.concatenate([hw[rows_ref[3 * c + i]] for i in range(3)], axis=1)
            z = jnp.dot(left, t_ref[c], preferred_element_type=F32)
            a = jnp.tanh(z * scale)
            act[k, c] = 1.0 - a * a
            fout[k, c] = (hbuf[k, c].astype(F32) + a).astype(BF16)
            if (c + 1) % per == 0:
                @pl.when(sec < sections - 1)
                def _(j=c // per):
                    fcopy(k, j).start()
        return carry

    lax.fori_loop(0, nmb, forward, 0)

    def backward(k, carry):
        @pl.when(final)
        def _():
            gbuf[k] = og_ref[k]

        @pl.when(sec < sections - 1)
        def _():
            bwhole(k).wait_recv()

        for c in range(nb):
            dz = (gbuf[k, c].astype(F32) * act[k, c]).astype(BF16)
            dz_ref[k, c] = dz
            back = lax.dot_general(dz, t_ref[c], (((1,), (1,)), ((), ())), preferred_element_type=F32)
            for i in range(3):
                prod[3 * c + i] = back[:, i * 128:(i + 1) * 128]
        scale = scl[k]
        acc = jnp.zeros((MB, 128), F32)
        for i in range(3 * nb):
            acc = acc * keep_ref[i] + prod[perm_ref[i]]
            pref[i] = acc
        inner = jnp.zeros((MB, 128), F32)
        for b in range(nb):
            q = hbuf[k, b].astype(F32) * scale
            u_ref[k, b] = q.astype(BF16)
            v = pref[last_ref[b]] * full_ref[b]
            inner = inner + v * q
            hw2 = v
            prod[b] = hw2
        inner = jnp.sum(inner, axis=1, keepdims=True) * (1.0 / width)
        inner = jnp.broadcast_to(inner, (MB, 128))
        for b in range(nb):
            q = hbuf[k, b].astype(F32) * scale
            g = gbuf[k, b].astype(F32) + scale * (prod[b] - q * inner)
            gout[k, b] = g.astype(BF16)
            if (b + 1) % per == 0:
                @pl.when(sec > 0)
                def _(j=b // per):
                    bcopy(k, j).start()
        return carry

    lax.fori_loop(0, nmb, backward, 0)

    def drain(k, carry):
        @pl.when(sec < sections - 1)
        def _():
            fwhole(k).wait_send()

        @pl.when(sec > 0)
        def _():
            bwhole(k).wait_send()

        return carry

    lax.fori_loop(0, nmb, drain, 0)


def reduce_kernel(gx, gy, nb, nmb, rows_ref, u_ref, dz_ref, out_ref,
                  ut, dzl, own, other, got0, sx, got1, sy, got2,
                  s0, r0, s1, r1, s2, r2):
    nt = 3 * nb
    ni = 128 // (2 * gx * gy)
    rx = gy * ni
    per = nt // GROUPS
    sub = per // 8
    dp = lax.axis_index("dp")
    me_c = lax.rem(dp, 2)
    me_x = lax.rem(dp // 2, gx)
    me_y = dp // (2 * gx)

    def at(y, x, c):
        return {"dp": (y * gx + x) * 2 + c}

    mate = at(me_y, me_x, 1 - me_c)
    xs = [at(me_y, lax.rem(me_x + j, gx), me_c) for j in range(1, gx)]
    ys = [at(lax.rem(me_y + j, gy), me_x, me_c) for j in range(1, gy)]

    barrier = pltpu.get_barrier_semaphore()
    for peer in [mate] + xs + ys:
        pl.semaphore_signal(barrier, inc=1, device_id=peer, device_id_type=MESH)

    p = lax.broadcasted_iota(jnp.int32, (128, 128), 0)
    r = lax.broadcasted_iota(jnp.int32, (128, 128), 1)
    far = p // 64
    core = far + me_c - 2 * far * me_c
    px = lax.rem(p // rx, gx)
    py = lax.rem(p // ni, gy)
    want = ((py * gx + px) * 2 + core) * ni + lax.rem(p, ni)
    order = jnp.where(r == want, 1.0, 0.0).astype(BF16)

    def prepare(b, carry):
        u = u_ref[:, b].astype(F32).reshape(nmb * MB, 128).astype(BF16)
        turned = lax.dot_general(order, u, (((1,), (1,)), ((), ())), preferred_element_type=F32)
        ut[b] = turned.astype(BF16)
        dzl[b] = dz_ref[:, b].astype(F32).reshape(nmb * MB, 128).astype(BF16)
        return carry

    lax.fori_loop(0, nb, prepare, 0)
    pl.semaphore_wait(barrier, gx + gy - 1)

    def copy0(g):
        return pltpu.make_async_remote_copy(
            src_ref=other.at[g], dst_ref=got0.at[g], send_sem=s0.at[g], recv_sem=r0.at[g],
            device_id=mate, device_id_type=MESH,
        )

    def copy1(g, j):
        return pltpu.make_async_remote_copy(
            src_ref=sx.at[g, j - 1], dst_ref=got1.at[g, j - 1], send_sem=s1.at[g, j - 1], recv_sem=r1.at[g, j - 1],
            device_id=xs[j - 1], device_id_type=MESH,
        )

    def copy2(g, j):
        return pltpu.make_async_remote_copy(
            src_ref=sy.at[g, lax.rem(me_y + j, gy)], dst_ref=got2.at[g, j - 1],
            send_sem=s2.at[g, j - 1], recv_sem=r2.at[g, j - 1],
            device_id=ys[j - 1], device_id_type=MESH,
        )

    for g in range(GROUPS):
        def column(c, carry, g=g):
            col = g * (per // 3) + c
            d = dzl[col]
            for i in range(3):
                full = jnp.dot(ut[rows_ref[3 * col + i]], d, preferred_element_type=F32)
                for x in range(gx):
                    own[g, x, 3 * c + i] = full[x * rx:(x + 1) * rx]
                    other[g, x, 3 * c + i] = full[64 + x * rx:64 + (x + 1) * rx].astype(BF16)
            return carry

        lax.fori_loop(0, per // 3, column, 0)
        copy0(g).start()

    for g in range(GROUPS):
        copy0(g).wait_recv()
        for j in range(1, gx):
            dest = lax.rem(me_x + j, gx)

            def fold(t, carry, g=g, j=j, dest=dest):
                sx[g, j - 1, t] = (own[g, dest, t] + got0[g, dest, t].astype(F32)).astype(BF16)
                return carry

            lax.fori_loop(0, per, fold, 0, unroll=4)
            copy1(g, j).start()

    a = lax.broadcasted_iota(jnp.int32, (8 * rx, 8 * rx), 0)
    b = lax.broadcasted_iota(jnp.int32, (8 * rx, 8 * rx), 1)
    src = lax.rem(a, 8) * rx + (a // (8 * ni)) * ni + lax.rem(a // 8, ni)
    mix = jnp.where(b == src, 1.0, 0.0).astype(BF16)

    for g in range(GROUPS):
        for j in range(1, gx):
            copy1(g, j).wait_recv()

        def block(q, carry, g=g):
            pieces = []
            for t in range(8):
                s = own[g, me_x, q * 8 + t] + got0[g, me_x, q * 8 + t].astype(F32)
                for j in range(gx - 1):
                    s = s + got1[g, j, q * 8 + t].astype(F32)
                pieces.append(s)
            s = jnp.concatenate(pieces, axis=0).astype(BF16)
            moved = jnp.dot(mix, s, preferred_element_type=F32).astype(BF16)
            for y in range(gy):
                sy[g, y, q] = moved[y * 8 * ni:(y + 1) * 8 * ni]
            return carry

        lax.fori_loop(0, sub, block, 0)
        for j in range(1, gy):
            copy2(g, j).start()

    for g in range(GROUPS):
        for j in range(1, gy):
            copy2(g, j).wait_recv()
        for q in range(sub):
            s = sy[g, me_y, q].astype(F32)
            for j in range(gy - 1):
                s = s + got2[g, j, q].astype(F32)
            for i in range(ni):
                out_ref[i, (g * sub + q) * 8:(g * sub + q + 1) * 8, :] = s[i * 8:(i + 1) * 8]

    for g in range(GROUPS):
        copy0(g).wait_send()
        for j in range(1, gx):
            copy1(g, j).wait_send()
        for j in range(1, gy):
            copy2(g, j).wait_send()


def tables(rows, nb):
    nt = rows.shape[0]
    spot = jnp.arange(nt, dtype=jnp.int32)
    before = (rows[None, :] < rows[:, None]) | ((rows[None, :] == rows[:, None]) & (spot[None, :] < spot[:, None]))
    rank = jnp.sum(before.astype(jnp.int32), axis=1)
    perm = jnp.sum(jnp.where(rank[None, :] == spot[:, None], spot[None, :], 0), axis=1)
    ordered = jnp.sum(jnp.where(rank[None, :] == spot[:, None], rows[None, :], 0), axis=1)
    previous = jnp.sum(jnp.where(rank[None, :] == spot[:, None] - 1, rows[None, :] + 1, 0), axis=1) - 1
    keep = jnp.where(ordered == previous, 1.0, 0.0).astype(F32)
    place = jnp.arange(nb, dtype=jnp.int32)
    upto = jnp.sum((rows[None, :] <= place[:, None]).astype(jnp.int32), axis=1)
    count = jnp.sum((rows[None, :] == place[:, None]).astype(jnp.int32), axis=1)
    return perm, jnp.maximum(upto - 1, 0), keep, (count > 0).astype(F32)


def local(gx, gy, inputs, tiles, tile_rows, out_grad):
    sections = lax.axis_size("section")
    rows = tile_rows[0]
    total, width = inputs.shape
    nb = width // 128
    nt = tiles.shape[1]
    nmb = total // MB
    feed = inputs.reshape(nmb, MB, nb, 128).transpose(0, 2, 1, 3)
    seeds = out_grad.reshape(nmb, MB, nb, 128).transpose(0, 2, 1, 3)
    tall = tiles.reshape(nb, 3 * 128, 128)
    perm, last, keep, full = tables(rows, nb)
    smem = pl.BlockSpec(memory_space=pltpu.SMEM)
    vmem = pl.BlockSpec(memory_space=pltpu.VMEM)
    dma = pltpu.SemaphoreType.DMA
    piece = (nmb, nb, MB, 128)
    u, dz = pl.pallas_call(
        functools.partial(relay_kernel, sections, nmb, nb),
        out_shape=[jax.ShapeDtypeStruct(piece, BF16), jax.ShapeDtypeStruct(piece, BF16)],
        in_specs=[smem] * 5 + [vmem] * 3,
        out_specs=[vmem] * 2,
        scratch_shapes=[
            pltpu.VMEM(piece, BF16), pltpu.VMEM(piece, BF16), pltpu.VMEM(piece, BF16), pltpu.VMEM(piece, BF16),
            pltpu.VMEM((nb, MB, 128), BF16),
            pltpu.VMEM(piece, F32),
            pltpu.VMEM((nmb, MB, 128), F32),
            pltpu.VMEM((nt, MB, 128), F32),
            pltpu.VMEM((nt, MB, 128), F32),
            dma((nmb,)), dma((nmb,)), dma((nmb,)), dma((nmb,)),
        ],
        compiler_params=pltpu.CompilerParams(collective_id=0, has_side_effects=True),
        name="relay",
    )(rows, perm, last, keep, full, feed, tall, seeds)
    ni = 128 // (2 * gx * gy)
    rx = gy * ni
    per = nt // GROUPS
    return pl.pallas_call(
        functools.partial(reduce_kernel, gx, gy, nb, nmb),
        out_shape=jax.ShapeDtypeStruct((ni, nt, 128), F32),
        in_specs=[smem] + [vmem] * 2,
        out_specs=vmem,
        scratch_shapes=[
            pltpu.VMEM((nb, 128, nmb * MB), BF16),
            pltpu.VMEM((nb, nmb * MB, 128), BF16),
            pltpu.VMEM((GROUPS, gx, per, rx, 128), F32),
            pltpu.VMEM((GROUPS, gx, per, rx, 128), BF16),
            pltpu.VMEM((GROUPS, gx, per, rx, 128), BF16),
            pltpu.VMEM((GROUPS, gx - 1, per, rx, 128), BF16),
            pltpu.VMEM((GROUPS, gx - 1, per, rx, 128), BF16),
            pltpu.VMEM((GROUPS, gy, per // 8, 8 * ni, 128), BF16),
            pltpu.VMEM((GROUPS, gy - 1, per // 8, 8 * ni, 128), BF16),
            dma((GROUPS,)), dma((GROUPS,)),
            dma((GROUPS, gx - 1)), dma((GROUPS, gx - 1)),
            dma((GROUPS, gy - 1)), dma((GROUPS, gy - 1)),
        ],
        compiler_params=pltpu.CompilerParams(collective_id=1, has_side_effects=True),
        name="reduce",
    )(rows, u, dz).reshape(ni, 1, nt, 128)


def solution(mesh, gx=GRID_X, gy=GRID_Y):
    return jax.shard_map(
        functools.partial(local, gx, gy),
        mesh=mesh,
        in_specs=(P("dp", None), P("section", None, None, None), P("section", None), P("dp", None)),
        out_specs=P("dp", "section", None, None),
        check_vma=False,
    )
```

time: 728 us -> 208 us (0.29)
  waiting for transfers between devices: 497 us -> 0 us
  Pallas kernels: 0 us -> 199 us
  starting transfers between devices: 129 us -> 0 us
  local copies, waits for them, and re-layouts: 33.4 us -> 1.52 us
  other arithmetic: 34.5 us -> 5.37 us
  matrix products: 16.5 us -> 0 us
  between operations: 13.5 us -> 0.03 us
    ppermute x38 -> x0, waiting for transfers between devices: 329 us -> none  [from_behind(): return lax.ppermute(array, axis, pairs)]
    pallas_call x0 -> x2, Pallas kernels: none -> 199 us  [the longest x1 166 us: local(): pl.pallas_call(functools.partial(relay_kernel, sections, nmb, nb), out_sh...]
    unnamed x2 -> x0, waiting for transfers between devices: 168 us -> none
    ppermute x38 -> x0, starting transfers between devices: 129 us -> none  [from_behind(): return lax.ppermute(array, axis, pairs)]
    dot_general x13 -> x0, matrix products: 16.5 us -> none  [the longest x4 5.83 us: layer_backward(): jnp.einsum('mtr,tb->mbr', back.reshape(count, nb * kpc, blk), onehot, pre...]
    dynamic_update_slice x8 -> x0, other arithmetic: 13.7 us -> none  [the longest x4 7.06 us: backward_work(): store_dz = lax.dynamic_update_index_in_dim(store_dz, dz, index, 0)]
    broadcast_in_dim x37 -> x0, local copies, waits for them, and re-layouts: 12.2 us -> none  [the longest x32 10.5 us: local(): blank = jnp.zeros((group_rows, width), jnp.bfloat16)]
  transfers between devices with their start and end apart: 39 -> 0, of which waited for: 39 -> 0; matrix products, arithmetic and copies ran while one was open for 0% -> 0% of each run, Pallas kernels for 0% -> 0%
where the time goes in v1:
time: 208 us; the launch traced here: 206 us
  Pallas kernels  199 us (96%)
  other arithmetic  5.37 us (3%)
    pallas_call x1, Pallas kernels, local(): pl.pallas_call(functools.partial(relay_kernel, sections, nmb, nb), out_sh...  166 us
    pallas_call x1, Pallas kernels, local(): pl.pallas_call(functools.partial(reduce_kernel, gx, gy, nb, nmb), out_sha...  33.4 us

profile of v1, /device:TPU:6, one launch (start us, length us, event | category | flops | bytes accessed | tf_op | source)
XLA Modules:
  0.0 206.0 jit_solution(7754973366793259015)
XLA Ops:
  0.0 0.9 convert_reduce_fusion
  0.9 0.7 add_bitcast_fusion
  1.6 1.4 select_reduce_fusion
  2.9 0.6 compare_select_fusion.keep_ref
  3.5 0.8 convert_reduce_fusion.1
  4.3 0.5 compare_convert_fusion.full_ref
  4.8 0.5 add_maximum_fusion.last_ref
  5.4 165.7 %relay.1 = (bf16[16,24,8,128]{3,2,1,0:T(8,128)(2,1)}, bf16[16,24,8,128]{3,2,1,0:T(8,128)(2,1)}) custom-call(s32[72]{0:T(128)} %bitcast.20, s32[72]{0:T(128)} %get-tuple-element.13.perm_ref, s32[24]{0:T(128)} %add_maximum_fusion.last_ref, f32[72]{0:T(128)} %compare_select_fusion.keep_ref, f32[24]{0:T(128)} %compare_convert_fusion.full_ref, ...), custom_call_target="tpu_custom_call" | custom-call | tf_op jit(solution)/shard_map/relay/pallas_call | solution.py:328
  171.0 33.4 %reduce.1 = f32[2,72,128]{2,1,0:T(8,128)} custom-call(s32[72]{0:T(128)} %bitcast.21, bf16[16,24,8,128]{3,2,1,0:T(8,128)(2,1)} %get-tuple-element.7.u_ref, bf16[16,24,8,128]{3,2,1,0:T(8,128)(2,1)} %get-tuple-element.8.dz_ref), custom_call_target="tpu_custom_call" | custom-call | tf_op jit(solution)/shard_map/reduce/pallas_call | solution.py:348
  204.4 1.5 copy.8
  (1 shorter events, 0.0 us)

commit v2 on v1

--- a/solution.py
+++ b/solution.py
@@ -10,6 +10,8 @@
 EPS = 1e-06
 MB = 8
 CHUNKS = 2
+CHAINS = 2
+AHEAD = 6
 GRID_X = 4
 GRID_Y = 8
 GROUPS = 3
@@ -18,13 +20,29 @@
 BF16 = jnp.bfloat16
 
 
-def relay_kernel(sections, nmb, nb, rows_ref, perm_ref, last_ref, keep_ref, full_ref, x_ref, t_ref, og_ref,
-                 u_ref, dz_ref,
-                 hbuf, gbuf, fout, gout, hw, act, scl, prod, pref,
+def arrange(gx, gy):
+    ni = 128 // (2 * gx * gy)
+    rx = gy * ni
+    side = lax.rem(lax.axis_index("dp"), 2)
+    p = lax.broadcasted_iota(jnp.int32, (128, 128), 0)
+    r = lax.broadcasted_iota(jnp.int32, (128, 128), 1)
+    far = p // 64
+    core = far + side - 2 * far * side
+    px = lax.rem(p // rx, gx)
+    py = lax.rem(p // ni, gy)
+    want = ((py * gx + px) * 2 + core) * ni + lax.rem(p, ni)
+    return jnp.where(r == want, 1.0, 0.0).astype(BF16)
+
+
+def relay_kernel(sections, nmb, nb, gx, gy, rows_ref, line_ref, x_ref, t_ref, og_ref,
+                 ut_ref, dz_ref,
+                 hbuf, gbuf, fout, gout, hw, act, scl, prod, pref, flip, board, table, tsem,
                  fsend, frecv, bsend, brecv):
     sec = lax.axis_index("section")
+    nt = 3 * nb
     width = nb * 128
     per = nb // CHUNKS
+    run = nt // CHAINS
     first = sec == 0
     final = sec == sections - 1
     up = jnp.minimum(sec + 1, sections - 1)
@@ -74,6 +92,52 @@
             src_ref=gout.at[k], dst_ref=gbuf.at[k], send_sem=bsend.at[k], recv_sem=brecv.at[k],
             device_id={"section": down}, device_id_type=MESH,
         )
+
+    def setup():
+        ia = lax.broadcasted_iota(jnp.int32, (nt, nt), 0)
+        ib = lax.broadcasted_iota(jnp.int32, (nt, nt), 1)
+        across = jnp.broadcast_to(line_ref[...], (nt, nt))
+        down_col = jnp.sum(jnp.where(ia == ib, across, 0), axis=1, keepdims=True)
+        along = jnp.broadcast_to(down_col, (nt, nt))
+        ahead = (across < along) | ((across == along) & (ib < ia))
+        rank = jnp.broadcast_to(jnp.sum(jnp.where(ahead, 1, 0), axis=1, keepdims=True), (nt, nt))
+        here = rank == ib
+        perm = jnp.sum(jnp.where(here, ia, 0), axis=0, keepdims=True)
+        ordered = jnp.sum(jnp.where(here, along, 0), axis=0, keepdims=True)
+        previous = jnp.sum(jnp.where(rank == ib - 1, along + 1, 0), axis=0, keepdims=True) - 1
+        upto = jnp.sum(jnp.where(along <= ib, 1, 0), axis=0, keepdims=True)
+        count = jnp.sum(jnp.where(along == ib, 1, 0), axis=0, keepdims=True)
+        last = jnp.maximum(upto - 1, 0)
+        board[0:1, 0:nt] = perm
+        board[1:2, 0:nt] = jnp.where(ordered == previous, 1, 0)
+        board[2:3, 0:nt] = last
+        board[3:4, 0:nt] = jnp.where(count > 0, 1, 0)
+        for j in range(CHAINS - 1):
+            end = run * j + run - 1
+            spans = (count > 0) & (upto - count <= end) & (last > end)
+            board[4 + j:5 + j, 0:nt] = jnp.where(spans, 1, 0)
+        copy = pltpu.make_async_copy(board, table, tsem)
+        copy.start()
+
+        def turn(c, carry):
+            for i in range(3):
+                flip[c, :, i * 128:(i + 1) * 128] = t_ref[c, i * 128:(i + 1) * 128, :].T
+            return carry
+
+        lax.fori_loop(0, nb, turn, 0)
+        copy.wait()
+
+    def turned():
+        order = arrange(gx, gy)
+
+        def one(b, carry):
+            q = hbuf[:, b].astype(F32) * scl[...]
+            u = q.reshape(nmb * MB, 128).astype(BF16)
+            moved = lax.dot_general(order, u, (((1,), (1,)), ((), ())), preferred_element_type=F32)
+            ut_ref[b] = moved.astype(BF16)
+            return carry
+
+        lax.fori_loop(0, nb, one, 0)
 
     def forward(k, carry):
         @pl.when(first)
@@ -105,8 +169,6 @@
                     fcopy(k, j).start()
         return carry
 
-    lax.fori_loop(0, nmb, forward, 0)
-
     def backward(k, carry):
         @pl.when(final)
         def _():
@@ -119,22 +181,24 @@
         for c in range(nb):
             dz = (gbuf[k, c].astype(F32) * act[k, c]).astype(BF16)
             dz_ref[k, c] = dz
-            back = lax.dot_general(dz, t_ref[c], (((1,), (1,)), ((), ())), preferred_element_type=F32)
+            back = jnp.dot(dz, flip[c], preferred_element_type=F32)
             for i in range(3):
                 prod[3 * c + i] = back[:, i * 128:(i + 1) * 128]
         scale = scl[k]
-        acc = jnp.zeros((MB, 128), F32)
-        for i in range(3 * nb):
-            acc = acc * keep_ref[i] + prod[perm_ref[i]]
-            pref[i] = acc
+        for j in range(CHAINS):
+            acc = prod[table[0, run * j]]
+            pref[run * j] = acc
+            for i in range(run * j + 1, run * j + run):
+                acc = acc * table[1, i].astype(F32) + prod[table[0, i]]
+                pref[i] = acc
         inner = jnp.zeros((MB, 128), F32)
         for b in range(nb):
             q = hbuf[k, b].astype(F32) * scale
-            u_ref[k, b] = q.astype(BF16)
-            v = pref[last_ref[b]] * full_ref[b]
+            v = pref[table[2, b]] * table[3, b].astype(F32)
+            for j in range(CHAINS - 1):
+                v = v + pref[run * j + run - 1] * table[4 + j, b].astype(F32)
             inner = inner + v * q
-            hw2 = v
-            prod[b] = hw2
+            prod[b] = v
         inner = jnp.sum(inner, axis=1, keepdims=True) * (1.0 / width)
         inner = jnp.broadcast_to(inner, (MB, 128))
         for b in range(nb):
@@ -147,7 +211,31 @@
                     bcopy(k, j).start()
         return carry
 
-    lax.fori_loop(0, nmb, backward, 0)
+    early = sec >= sections // 2
+    warm = jnp.minimum(1 + AHEAD * (sections - 1 - sec), nmb)
+
+    @pl.when(early)
+    def _():
+        setup()
+
+    lax.fori_loop(0, warm, forward, 0)
+
+    @pl.when(jnp.logical_not(early))
+    def _():
+        setup()
+        turned()
+
+    def both(k, carry):
+        backward(k, carry)
+        forward(k + warm, carry)
+        return carry
+
+    lax.fori_loop(0, nmb - warm, both, 0)
+    lax.fori_loop(nmb - warm, nmb, backward, 0)
+
+    @pl.when(early)
+    def _():
+        turned()
 
     def drain(k, carry):
         @pl.when(sec < sections - 1)
@@ -163,13 +251,14 @@
     lax.fori_loop(0, nmb, drain, 0)
 
 
-def reduce_kernel(gx, gy, nb, nmb, rows_ref, u_ref, dz_ref, out_ref,
-                  ut, dzl, own, other, got0, sx, got1, sy, got2,
+def reduce_kernel(gx, gy, nb, nmb, rows_ref, ut_ref, dz_ref, out_ref,
+                  dzl, own, other, got0, so, sr, sl, ro, got1, sy, got2,
                   s0, r0, s1, r1, s2, r2):
     nt = 3 * nb
     ni = 128 // (2 * gx * gy)
     rx = gy * ni
     per = nt // GROUPS
+    half = per // 2
     sub = per // 8
     dp = lax.axis_index("dp")
     me_c = lax.rem(dp, 2)
@@ -179,32 +268,24 @@
     def at(y, x, c):
         return {"dp": (y * gx + x) * 2 + c}
 
+    x_right = lax.rem(me_x + 1, gx)
+    x_left = lax.rem(me_x + gx - 1, gx)
+    x_over = lax.rem(me_x + 2, gx)
     mate = at(me_y, me_x, 1 - me_c)
-    xs = [at(me_y, lax.rem(me_x + j, gx), me_c) for j in range(1, gx)]
+    right = at(me_y, x_right, me_c)
+    left = at(me_y, x_left, me_c)
     ys = [at(lax.rem(me_y + j, gy), me_x, me_c) for j in range(1, gy)]
 
     barrier = pltpu.get_barrier_semaphore()
-    for peer in [mate] + xs + ys:
+    for peer in [mate, right, left] + ys:
         pl.semaphore_signal(barrier, inc=1, device_id=peer, device_id_type=MESH)
 
-    p = lax.broadcasted_iota(jnp.int32, (128, 128), 0)
-    r = lax.broadcasted_iota(jnp.int32, (128, 128), 1)
-    far = p // 64
-    core = far + me_c - 2 * far * me_c
-    px = lax.rem(p // rx, gx)
-    py = lax.rem(p // ni, gy)
-    want = ((py * gx + px) * 2 + core) * ni + lax.rem(p, ni)
-    order = jnp.where(r == want, 1.0, 0.0).astype(BF16)
-
     def prepare(b, carry):
-        u = u_ref[:, b].astype(F32).reshape(nmb * MB, 128).astype(BF16)
-        turned = lax.dot_general(order, u, (((1,), (1,)), ((), ())), preferred_element_type=F32)
-        ut[b] = turned.astype(BF16)
         dzl[b] = dz_ref[:, b].astype(F32).reshape(nmb * MB, 128).astype(BF16)
         return carry
 
     lax.fori_loop(0, nb, prepare, 0)
-    pl.semaphore_wait(barrier, gx + gy - 1)
+    pl.semaphore_wait(barrier, gy + 2)
 
     def copy0(g):
         return pltpu.make_async_remote_copy(
@@ -212,10 +293,20 @@
             device_id=mate, device_id_type=MESH,
         )
 
-    def copy1(g, j):
-        return pltpu.make_async_remote_copy(
-            src_ref=sx.at[g, j - 1], dst_ref=got1.at[g, j - 1], send_sem=s1.at[g, j - 1], recv_sem=r1.at[g, j - 1],
-            device_id=xs[j - 1], device_id_type=MESH,
+    low, high = pl.ds(0, half), pl.ds(half, half)
+
+    def copy1(g, kind):
+        src, dst, peer = (
+            (so.at[g, low], ro.at[g, 0], right),
+            (so.at[g, high], ro.at[g, 1], left),
+            (sr.at[g, high], got1.at[g, 0, high], right),
+            (sl.at[g, low], got1.at[g, 1, low], left),
+            (sr.at[g, low], got1.at[g, 0, low], right),
+            (sl.at[g, high], got1.at[g, 1, high], left),
+        )[kind]
+        return pltpu.make_async_remote_copy(
+            src_ref=src, dst_ref=dst, send_sem=s1.at[g, kind], recv_sem=r1.at[g, kind],
+            device_id=peer, device_id_type=MESH,
         )
 
     def copy2(g, j):
@@ -230,7 +321,7 @@
             col = g * (per // 3) + c
             d = dzl[col]
             for i in range(3):
-                full = jnp.dot(ut[rows_ref[3 * col + i]], d, preferred_element_type=F32)
+                full = jnp.dot(ut_ref[rows_ref[3 * col + i]], d, preferred_element_type=F32)
                 for x in range(gx):
                     own[g, x, 3 * c + i] = full[x * rx:(x + 1) * rx]
                     other[g, x, 3 * c + i] = full[64 + x * rx:64 + (x + 1) * rx].astype(BF16)
@@ -239,17 +330,40 @@
         lax.fori_loop(0, per // 3, column, 0)
         copy0(g).start()
 
+    def both(g, x, t):
+        return own[g, x, t] + got0[g, x, t].astype(F32)
+
     for g in range(GROUPS):
         copy0(g).wait_recv()
-        for j in range(1, gx):
-            dest = lax.rem(me_x + j, gx)
-
-            def fold(t, carry, g=g, j=j, dest=dest):
-                sx[g, j - 1, t] = (own[g, dest, t] + got0[g, dest, t].astype(F32)).astype(BF16)
-                return carry
-
-            lax.fori_loop(0, per, fold, 0, unroll=4)
-            copy1(g, j).start()
+
+        def over(t, carry, g=g):
+            so[g, t] = both(g, x_over, t).astype(BF16)
+            return carry
+
+        def straight(t, carry, g=g):
+            sr[g, half + t] = both(g, x_right, half + t).astype(BF16)
+            sl[g, t] = both(g, x_left, t).astype(BF16)
+            return carry
+
+        lax.fori_loop(0, per, over, 0, unroll=4)
+        copy1(g, 0).start()
+        copy1(g, 1).start()
+        lax.fori_loop(0, half, straight, 0, unroll=4)
+        copy1(g, 2).start()
+        copy1(g, 3).start()
+
+    for g in range(GROUPS):
+        copy1(g, 0).wait_recv()
+        copy1(g, 1).wait_recv()
+
+        def carried(t, carry, g=g):
+            sr[g, t] = (both(g, x_right, t) + ro[g, 0, t].astype(F32)).astype(BF16)
+            sl[g, half + t] = (both(g, x_left, half + t) + ro[g, 1, t].astype(F32)).astype(BF16)
+            return carry
+
+        lax.fori_loop(0, half, carried, 0, unroll=4)
+        copy1(g, 4).start()
+        copy1(g, 5).start()
 
     a = lax.broadcasted_iota(jnp.int32, (8 * rx, 8 * rx), 0)
     b = lax.broadcasted_iota(jnp.int32, (8 * rx, 8 * rx), 1)
@@ -257,14 +371,14 @@
     mix = jnp.where(b == src, 1.0, 0.0).astype(BF16)
 
     for g in range(GROUPS):
-        for j in range(1, gx):
-            copy1(g, j).wait_recv()
+        for kind in range(2, 6):
+            copy1(g, kind).wait_recv()
 
         def block(q, carry, g=g):
             pieces = []
             for t in range(8):
-                s = own[g, me_x, q * 8 + t] + got0[g, me_x, q * 8 + t].astype(F32)
-                for j in range(gx - 1):
+                s = both(g, me_x, q * 8 + t)
+                for j in range(2):
                     s = s + got1[g, j, q * 8 + t].astype(F32)
                 pieces.append(s)
             s = jnp.concatenate(pieces, axis=0).astype(BF16)
@@ -289,25 +403,10 @@
 
     for g in range(GROUPS):
         copy0(g).wait_send()
-        for j in range(1, gx):
-            copy1(g, j).wait_send()
+        for kind in range(6):
+            copy1(g, kind).wait_send()
         for j in range(1, gy):
             copy2(g, j).wait_send()
-
-
-def tables(rows, nb):
-    nt = rows.shape[0]
-    spot = jnp.arange(nt, dtype=jnp.int32)
-    before = (rows[None, :] < rows[:, None]) | ((rows[None, :] == rows[:, None]) & (spot[None, :] < spot[:, None]))
-    rank = jnp.sum(before.astype(jnp.int32), axis=1)
-    perm = jnp.sum(jnp.where(rank[None, :] == spot[:, None], spot[None, :], 0), axis=1)
-    ordered = jnp.sum(jnp.where(rank[None, :] == spot[:, None], rows[None, :], 0), axis=1)
-    previous = jnp.sum(jnp.where(rank[None, :] == spot[:, None] - 1, rows[None, :] + 1, 0), axis=1) - 1
-    keep = jnp.where(ordered == previous, 1.0, 0.0).astype(F32)
-    place = jnp.arange(nb, dtype=jnp.int32)
-    upto = jnp.sum((rows[None, :] <= place[:, None]).astype(jnp.int32), axis=1)
-    count = jnp.sum((rows[None, :] == place[:, None]).astype(jnp.int32), axis=1)
-    return perm, jnp.maximum(upto - 1, 0), keep, (count > 0).astype(F32)
 
 
 def local(gx, gy, inputs, tiles, tile_rows, out_grad):
@@ -320,15 +419,14 @@
     feed = inputs.reshape(nmb, MB, nb, 128).transpose(0, 2, 1, 3)
     seeds = out_grad.reshape(nmb, MB, nb, 128).transpose(0, 2, 1, 3)
     tall = tiles.reshape(nb, 3 * 128, 128)
-    perm, last, keep, full = tables(rows, nb)
     smem = pl.BlockSpec(memory_space=pltpu.SMEM)
     vmem = pl.BlockSpec(memory_space=pltpu.VMEM)
     dma = pltpu.SemaphoreType.DMA
     piece = (nmb, nb, MB, 128)
-    u, dz = pl.pallas_call(
-        functools.partial(relay_kernel, sections, nmb, nb),
-        out_shape=[jax.ShapeDtypeStruct(piece, BF16), jax.ShapeDtypeStruct(piece, BF16)],
-        in_specs=[smem] * 5 + [vmem] * 3,
+    ut, dz = pl.pallas_call(
+        functools.partial(relay_kernel, sections, nmb, nb, gx, gy),
+        out_shape=[jax.ShapeDtypeStruct((nb, 128, nmb * MB), BF16), jax.ShapeDtypeStruct(piece, BF16)],
+        in_specs=[smem] + [vmem] * 4,
         out_specs=[vmem] * 2,
         scratch_shapes=[
             pltpu.VMEM(piece, BF16), pltpu.VMEM(piece, BF16), pltpu.VMEM(piece, BF16), pltpu.VMEM(piece, BF16),
@@ -337,11 +435,15 @@
             pltpu.VMEM((nmb, MB, 128), F32),
             pltpu.VMEM((nt, MB, 128), F32),
             pltpu.VMEM((nt, MB, 128), F32),
+            pltpu.VMEM((nb, 128, 3 * 128), BF16),
+            pltpu.VMEM((8, 128), jnp.int32),
+            pltpu.SMEM((8, 128), jnp.int32),
+            dma(()),
             dma((nmb,)), dma((nmb,)), dma((nmb,)), dma((nmb,)),
         ],
         compiler_params=pltpu.CompilerParams(collective_id=0, has_side_effects=True),
         name="relay",
-    )(rows, perm, last, keep, full, feed, tall, seeds)
+    )(rows, tile_rows, feed, tall, seeds)
     ni = 128 // (2 * gx * gy)
     rx = gy * ni
     per = nt // GROUPS
@@ -351,22 +453,24 @@
         in_specs=[smem] + [vmem] * 2,
         out_specs=vmem,
         scratch_shapes=[
-            pltpu.VMEM((nb, 128, nmb * MB), BF16),
             pltpu.VMEM((nb, nmb * MB, 128), BF16),
             pltpu.VMEM((GROUPS, gx, per, rx, 128), F32),
             pltpu.VMEM((GROUPS, gx, per, rx, 128), BF16),
             pltpu.VMEM((GROUPS, gx, per, rx, 128), BF16),
-            pltpu.VMEM((GROUPS, gx - 1, per, rx, 128), BF16),
-            pltpu.VMEM((GROUPS, gx - 1, per, rx, 128), BF16),
+            pltpu.VMEM((GROUPS, per, rx, 128), BF16),
+            pltpu.VMEM((GROUPS, per, rx, 128), BF16),
+            pltpu.VMEM((GROUPS, per, rx, 128), BF16),
+            pltpu.VMEM((GROUPS, 2, per // 2, rx, 128), BF16),
+            pltpu.VMEM((GROUPS, 2, per, rx, 128), BF16),
             pltpu.VMEM((GROUPS, gy, per // 8, 8 * ni, 128), BF16),
             pltpu.VMEM((GROUPS, gy - 1, per // 8, 8 * ni, 128), BF16),
             dma((GROUPS,)), dma((GROUPS,)),
-            dma((GROUPS, gx - 1)), dma((GROUPS, gx - 1)),
+            dma((GROUPS, 6)), dma((GROUPS, 6)),
             dma((GROUPS, gy - 1)), dma((GROUPS, gy - 1)),
         ],
         compiler_params=pltpu.CompilerParams(collective_id=1, has_side_effects=True),
         name="reduce",
-    )(rows, u, dz).reshape(ni, 1, nt, 128)
+    )(rows, ut, dz).reshape(ni, 1, nt, 128)
 
 
 def solution(mesh, gx=GRID_X, gy=GRID_Y):

time: 208 us -> 184 us (0.88)
  Pallas kernels: 199 us -> 182 us
  other arithmetic: 5.37 us -> 0 us
    pallas_call x1, Pallas kernels: 166 us -> 148 us  [local(): pl.pallas_call(functools.partial(relay_kernel, sections, nmb, nb, gx, gy)...]
    reduce_sum x3 -> x0, other arithmetic: 3.03 us -> none  [the longest x1 1.35 us: tables(): jnp.sum(jnp.where(rank[None, :] == spot[:, None] - 1, rows[None, :] + 1,...]
where the time goes in v2:
time: 184 us
  Pallas kernels  182 us (99%)
    pallas_call x1, Pallas kernels, local(): pl.pallas_call(functools.partial(relay_kernel, sections, nmb, nb, gx, gy)...  148 us
    pallas_call x1, Pallas kernels, local(): pl.pallas_call(functools.partial(reduce_kernel, gx, gy, nb, nmb), out_sha...  34.7 us

profile of v2, /device:TPU:6, one launch (start us, length us, event | category | flops | bytes accessed | tf_op | source)
XLA Modules:
  0.0 183.8 jit_solution(5783724674941935921)
XLA Ops:
  0.0 147.6 %relay.1 = (bf16[24,128,128]{2,1,0:T(8,128)(2,1)}, bf16[16,24,8,128]{3,2,1,0:T(8,128)(2,1)}) custom-call(s32[72]{0:T(128)} %bitcast.15, s32[1,72]{1,0:T(1,128)} %line_ref.1, bf16[16,24,8,128]{3,2,1,0:T(8,128)(2,1)} %bitcast.12, bf16[24,384,128]{2,1,0:T(8,128)(2,1)} %bitcast.11, bf16[16,24,8,128]{3,2,1,0:T(8,128)(2,1)} %bitcast.13), custom_call_target="tpu_custom_call" | custom-call | tf_op jit(solution)/shard_map/relay/pallas_call | solution.py:426
  147.6 34.7 %reduce.1 = f32[2,72,128]{2,1,0:T(8,128)} custom-call(s32[72]{0:T(128)} %bitcast.16, bf16[24,128,128]{2,1,0:T(8,128)(2,1)} %get-tuple-element.7.ut_ref, bf16[16,24,8,128]{3,2,1,0:T(8,128)(2,1)} %get-tuple-element.8.dz_ref), custom_call_target="tpu_custom_call" | custom-call | tf_op jit(solution)/shard_map/reduce/pallas_call | solution.py:450
  182.3 1.5 copy.7

commit v3 on v2

--- a/solution.py
+++ b/solution.py
@@ -35,9 +35,10 @@
 
 
 def relay_kernel(sections, nmb, nb, gx, gy, rows_ref, line_ref, x_ref, t_ref, og_ref,
-                 ut_ref, dz_ref,
+                 out_ref,
+                 dzo, dzg, uto, uts, utg, own, so, sr, sl, ro, got1, sy, got2,
                  hbuf, gbuf, fout, gout, hw, act, scl, prod, pref, flip, board, table, tsem,
-                 fsend, frecv, bsend, brecv):
+                 fsend, frecv, bsend, brecv, dsend, drecv, us, ur, s1, r1, s2, r2):
     sec = lax.axis_index("section")
     nt = 3 * nb
     width = nb * 128
@@ -45,21 +46,46 @@
     run = nt // CHAINS
     first = sec == 0
     final = sec == sections - 1
-    up = jnp.minimum(sec + 1, sections - 1)
-    down = jnp.maximum(sec - 1, 0)
+    dp = lax.axis_index("dp")
+    swap = dp + 1 - 2 * lax.rem(dp, 2)
+    straight = sections - 1 - lax.rem(sections - 1, 2)
+    up = {"dp": jnp.where(sec < straight, swap, dp), "section": jnp.minimum(sec + 1, sections - 1)}
+    down = {"dp": jnp.where(sec - 1 < straight, swap, dp), "section": jnp.maximum(sec - 1, 0)}
+
+    ni = 128 // (2 * gx * gy)
+    rx = gy * ni
+    tper = nt // GROUPS
+    half = tper // 2
+    sub = tper // 8
+    me_c = lax.rem(dp, 2)
+    me_x = lax.rem(dp // 2, gx)
+    me_y = dp // (2 * gx)
+
+    def at(y, x):
+        return {"dp": (y * gx + x) * 2 + me_c}
+
+    x_right = lax.rem(me_x + 1, gx)
+    x_left = lax.rem(me_x + gx - 1, gx)
+    x_over = lax.rem(me_x + 2, gx)
+    mate = {"dp": swap}
+    right = at(me_y, x_right)
+    left = at(me_y, x_left)
+    ys = [at(lax.rem(me_y + j, gy), me_x) for j in range(1, gy)]
 
     barrier = pltpu.get_barrier_semaphore()
 
     @pl.when(sec > 0)
     def _():
-        pl.semaphore_signal(barrier, inc=1, device_id={"section": down}, device_id_type=MESH)
+        pl.semaphore_signal(barrier, inc=1, device_id=down, device_id_type=MESH)
 
     @pl.when(sec < sections - 1)
     def _():
-        pl.semaphore_signal(barrier, inc=1, device_id={"section": up}, device_id_type=MESH)
-
-    near = jnp.where(first, 0, 1) + jnp.where(final, 0, 1)
-    pl.semaphore_wait(barrier, near)
+        pl.semaphore_signal(barrier, inc=1, device_id=up, device_id_type=MESH)
+
+    for peer in ys + [left, right, mate]:
+        pl.semaphore_signal(barrier, inc=1, device_id=peer, device_id_type=MESH)
+
+    pl.semaphore_wait(barrier, gy + 2 + jnp.where(first, 0, 1) + jnp.where(final, 0, 1))
 
     def fcopy(k, j):
         return pltpu.make_async_remote_copy(
@@ -67,7 +93,7 @@
             dst_ref=hbuf.at[k, pl.ds(j * per, per)],
             send_sem=fsend.at[k],
             recv_sem=frecv.at[k],
-            device_id={"section": up},
+            device_id=up,
             device_id_type=MESH,
         )
 
@@ -77,20 +103,31 @@
             dst_ref=gbuf.at[k, pl.ds(j * per, per)],
             send_sem=bsend.at[k],
             recv_sem=brecv.at[k],
-            device_id={"section": down},
+            device_id=down,
             device_id_type=MESH,
         )
 
     def fwhole(k):
         return pltpu.make_async_remote_copy(
             src_ref=fout.at[k], dst_ref=hbuf.at[k], send_sem=fsend.at[k], recv_sem=frecv.at[k],
-            device_id={"section": up}, device_id_type=MESH,
+            device_id=up, device_id_type=MESH,
         )
 
     def bwhole(k):
         return pltpu.make_async_remote_copy(
             src_ref=gout.at[k], dst_ref=gbuf.at[k], send_sem=bsend.at[k], recv_sem=brecv.at[k],
-            device_id={"section": down}, device_id_type=MESH,
+            device_id=down, device_id_type=MESH,
+        )
+
+    def dcopy(k):
+        return pltpu.make_async_remote_copy(
+            src_ref=dzo.at[k], dst_ref=dzg.at[k], send_sem=dsend.at[k], recv_sem=drecv.at[k],
+            device_id=mate, device_id_type=MESH,
+        )
+
+    def ucopy():
+        return pltpu.make_async_remote_copy(
+            src_ref=uts, dst_ref=utg, send_sem=us, recv_sem=ur, device_id=mate, device_id_type=MESH,
         )
 
     def setup():
@@ -134,10 +171,13 @@
             q = hbuf[:, b].astype(F32) * scl[...]
             u = q.reshape(nmb * MB, 128).astype(BF16)
             moved = lax.dot_general(order, u, (((1,), (1,)), ((), ())), preferred_element_type=F32)
-            ut_ref[b] = moved.astype(BF16)
+            moved = moved.astype(BF16)
+            uto[b] = moved[:64]
+            uts[b] = moved[64:]
             return carry
 
         lax.fori_loop(0, nb, one, 0)
+        ucopy().start()
 
     def forward(k, carry):
         @pl.when(first)
@@ -169,6 +209,13 @@
                     fcopy(k, j).start()
         return carry
 
+    def ending(k, carry):
+        bwhole(k).wait_recv()
+        for c in range(nb):
+            dzo[k, c] = (gbuf[k, c].astype(F32) * act[k, c]).astype(BF16)
+        dcopy(k).start()
+        return carry
+
     def backward(k, carry):
         @pl.when(final)
         def _():
@@ -180,7 +227,7 @@
 
         for c in range(nb):
             dz = (gbuf[k, c].astype(F32) * act[k, c]).astype(BF16)
-            dz_ref[k, c] = dz
+            dzo[k, c] = dz
             back = jnp.dot(dz, flip[c], preferred_element_type=F32)
             for i in range(3):
                 prod[3 * c + i] = back[:, i * 128:(i + 1) * 128]
@@ -206,9 +253,8 @@
             g = gbuf[k, b].astype(F32) + scale * (prod[b] - q * inner)
             gout[k, b] = g.astype(BF16)
             if (b + 1) % per == 0:
-                @pl.when(sec > 0)
-                def _(j=b // per):
-                    bcopy(k, j).start()
+                bcopy(k, b // per).start()
+        dcopy(k).start()
         return carry
 
     early = sec >= sections // 2
@@ -231,67 +277,26 @@
         return carry
 
     lax.fori_loop(0, nmb - warm, both, 0)
-    lax.fori_loop(nmb - warm, nmb, backward, 0)
+
+    @pl.when(sec > 0)
+    def _():
+        lax.fori_loop(nmb - warm, nmb, backward, 0)
+
+    @pl.when(first)
+    def _():
+        lax.fori_loop(0, nmb, ending, 0)
 
     @pl.when(early)
     def _():
         turned()
 
-    def drain(k, carry):
-        @pl.when(sec < sections - 1)
-        def _():
-            fwhole(k).wait_send()
-
-        @pl.when(sec > 0)
-        def _():
-            bwhole(k).wait_send()
-
-        return carry
-
-    lax.fori_loop(0, nmb, drain, 0)
-
-
-def reduce_kernel(gx, gy, nb, nmb, rows_ref, ut_ref, dz_ref, out_ref,
-                  dzl, own, other, got0, so, sr, sl, ro, got1, sy, got2,
-                  s0, r0, s1, r1, s2, r2):
-    nt = 3 * nb
-    ni = 128 // (2 * gx * gy)
-    rx = gy * ni
-    per = nt // GROUPS
-    half = per // 2
-    sub = per // 8
-    dp = lax.axis_index("dp")
-    me_c = lax.rem(dp, 2)
-    me_x = lax.rem(dp // 2, gx)
-    me_y = dp // (2 * gx)
-
-    def at(y, x, c):
-        return {"dp": (y * gx + x) * 2 + c}
-
-    x_right = lax.rem(me_x + 1, gx)
-    x_left = lax.rem(me_x + gx - 1, gx)
-    x_over = lax.rem(me_x + 2, gx)
-    mate = at(me_y, me_x, 1 - me_c)
-    right = at(me_y, x_right, me_c)
-    left = at(me_y, x_left, me_c)
-    ys = [at(lax.rem(me_y + j, gy), me_x, me_c) for j in range(1, gy)]
-
-    barrier = pltpu.get_barrier_semaphore()
-    for peer in [mate, right, left] + ys:
-        pl.semaphore_signal(barrier, inc=1, device_id=peer, device_id_type=MESH)
-
-    def prepare(b, carry):
-        dzl[b] = dz_ref[:, b].astype(F32).reshape(nmb * MB, 128).astype(BF16)
-        return carry
-
-    lax.fori_loop(0, nb, prepare, 0)
-    pl.semaphore_wait(barrier, gy + 2)
-
-    def copy0(g):
-        return pltpu.make_async_remote_copy(
-            src_ref=other.at[g], dst_ref=got0.at[g], send_sem=s0.at[g], recv_sem=r0.at[g],
-            device_id=mate, device_id_type=MESH,
-        )
+    ucopy().wait_recv()
+
+    def arrived(k, carry):
+        dcopy(k).wait_recv()
+        return carry
+
+    lax.fori_loop(0, nmb, arrived, 0)
 
     low, high = pl.ds(0, half), pl.ds(half, half)
 
@@ -318,34 +323,30 @@
 
     for g in range(GROUPS):
         def column(c, carry, g=g):
-            col = g * (per // 3) + c
-            d = dzl[col]
+            col = g * (tper // 3) + c
+            mine = dzo[:, col].astype(F32).reshape(nmb * MB, 128)
+            theirs = dzg[:, col].astype(F32).reshape(nmb * MB, 128)
+            d = jnp.concatenate([mine, theirs], axis=0).astype(BF16)
             for i in range(3):
-                full = jnp.dot(ut_ref[rows_ref[3 * col + i]], d, preferred_element_type=F32)
+                row = rows_ref[3 * col + i]
+                wide = jnp.concatenate([uto[row], utg[row]], axis=1)
+                full = jnp.dot(wide, d, preferred_element_type=F32)
                 for x in range(gx):
                     own[g, x, 3 * c + i] = full[x * rx:(x + 1) * rx]
-                    other[g, x, 3 * c + i] = full[64 + x * rx:64 + (x + 1) * rx].astype(BF16)
-            return carry
-
-        lax.fori_loop(0, per // 3, column, 0)
-        copy0(g).start()
-
-    def both(g, x, t):
-        return own[g, x, t] + got0[g, x, t].astype(F32)
-
-    for g in range(GROUPS):
-        copy0(g).wait_recv()
+            return carry
+
+        lax.fori_loop(0, tper // 3, column, 0)
 
         def over(t, carry, g=g):
-            so[g, t] = both(g, x_over, t).astype(BF16)
+            so[g, t] = own[g, x_over, t].astype(BF16)
             return carry
 
         def straight(t, carry, g=g):
-            sr[g, half + t] = both(g, x_right, half + t).astype(BF16)
-            sl[g, t] = both(g, x_left, t).astype(BF16)
-            return carry
-
-        lax.fori_loop(0, per, over, 0, unroll=4)
+            sr[g, half + t] = own[g, x_right, half + t].astype(BF16)
+            sl[g, t] = own[g, x_left, t].astype(BF16)
+            return carry
+
+        lax.fori_loop(0, tper, over, 0, unroll=4)
         copy1(g, 0).start()
         copy1(g, 1).start()
         lax.fori_loop(0, half, straight, 0, unroll=4)
@@ -357,8 +358,8 @@
         copy1(g, 1).wait_recv()
 
         def carried(t, carry, g=g):
-            sr[g, t] = (both(g, x_right, t) + ro[g, 0, t].astype(F32)).astype(BF16)
-            sl[g, half + t] = (both(g, x_left, half + t) + ro[g, 1, t].astype(F32)).astype(BF16)
+            sr[g, t] = (own[g, x_right, t] + ro[g, 0, t].astype(F32)).astype(BF16)
+            sl[g, half + t] = (own[g, x_left, half + t] + ro[g, 1, t].astype(F32)).astype(BF16)
             return carry
 
         lax.fori_loop(0, half, carried, 0, unroll=4)
@@ -377,7 +378,7 @@
         def block(q, carry, g=g):
             pieces = []
             for t in range(8):
-                s = both(g, me_x, q * 8 + t)
+                s = own[g, me_x, q * 8 + t]
                 for j in range(2):
                     s = s + got1[g, j, q * 8 + t].astype(F32)
                 pieces.append(s)
@@ -402,11 +403,25 @@
                 out_ref[i, (g * sub + q) * 8:(g * sub + q + 1) * 8, :] = s[i * 8:(i + 1) * 8]
 
     for g in range(GROUPS):
-        copy0(g).wait_send()
         for kind in range(6):
             copy1(g, kind).wait_send()
         for j in range(1, gy):
             copy2(g, j).wait_send()
+    ucopy().wait_send()
+
+    def drain(k, carry):
+        @pl.when(sec < sections - 1)
+        def _():
+            fwhole(k).wait_send()
+
+        @pl.when(sec > 0)
+        def _():
+            bwhole(k).wait_send()
+
+        dcopy(k).wait_send()
+        return carry
+
+    lax.fori_loop(0, nmb, drain, 0)
 
 
 def local(gx, gy, inputs, tiles, tile_rows, out_grad):
@@ -423,12 +438,26 @@
     vmem = pl.BlockSpec(memory_space=pltpu.VMEM)
     dma = pltpu.SemaphoreType.DMA
     piece = (nmb, nb, MB, 128)
-    ut, dz = pl.pallas_call(
+    ni = 128 // (2 * gx * gy)
+    rx = gy * ni
+    tper = nt // GROUPS
+    strip = (nb, 64, nmb * MB)
+    return pl.pallas_call(
         functools.partial(relay_kernel, sections, nmb, nb, gx, gy),
-        out_shape=[jax.ShapeDtypeStruct((nb, 128, nmb * MB), BF16), jax.ShapeDtypeStruct(piece, BF16)],
+        out_shape=jax.ShapeDtypeStruct((ni, nt, 128), F32),
         in_specs=[smem] + [vmem] * 4,
-        out_specs=[vmem] * 2,
+        out_specs=vmem,
         scratch_shapes=[
+            pltpu.VMEM(piece, BF16), pltpu.VMEM(piece, BF16),
+            pltpu.VMEM(strip, BF16), pltpu.VMEM(strip, BF16), pltpu.VMEM(strip, BF16),
+            pltpu.VMEM((GROUPS, gx, tper, rx, 128), F32),
+            pltpu.VMEM((GROUPS, tper, rx, 128), BF16),
+            pltpu.VMEM((GROUPS, tper, rx, 128), BF16),
+            pltpu.VMEM((GROUPS, tper, rx, 128), BF16),
+            pltpu.VMEM((GROUPS, 2, tper // 2, rx, 128), BF16),
+            pltpu.VMEM((GROUPS, 2, tper, rx, 128), BF16),
+            pltpu.VMEM((GROUPS, gy, tper // 8, 8 * ni, 128), BF16),
+            pltpu.VMEM((GROUPS, gy - 1, tper // 8, 8 * ni, 128), BF16),
             pltpu.VMEM(piece, BF16), pltpu.VMEM(piece, BF16), pltpu.VMEM(piece, BF16), pltpu.VMEM(piece, BF16),
             pltpu.VMEM((nb, MB, 128), BF16),
             pltpu.VMEM(piece, F32),
@@ -439,38 +468,14 @@
             pltpu.VMEM((8, 128), jnp.int32),
             pltpu.SMEM((8, 128), jnp.int32),
             dma(()),
-            dma((nmb,)), dma((nmb,)), dma((nmb,)), dma((nmb,)),
+            dma((nmb,)), dma((nmb,)), dma((nmb,)), dma((nmb,)), dma((nmb,)), dma((nmb,)),
+            dma(()), dma(()),
+            dma((GROUPS, 6)), dma((GROUPS, 6)),
+            dma((GROUPS, gy - 1)), dma((GROUPS, gy - 1)),
         ],
         compiler_params=pltpu.CompilerParams(collective_id=0, has_side_effects=True),
         name="relay",
-    )(rows, tile_rows, feed, tall, seeds)
-    ni = 128 // (2 * gx * gy)
-    rx = gy * ni
-    per = nt // GROUPS
-    return pl.pallas_call(
-        functools.partial(reduce_kernel, gx, gy, nb, nmb),
-        out_shape=jax.ShapeDtypeStruct((ni, nt, 128), F32),
-        in_specs=[smem] + [vmem] * 2,
-        out_specs=vmem,
-        scratch_shapes=[
-            pltpu.VMEM((nb, nmb * MB, 128), BF16),
-            pltpu.VMEM((GROUPS, gx, per, rx, 128), F32),
-            pltpu.VMEM((GROUPS, gx, per, rx, 128), BF16),
-            pltpu.VMEM((GROUPS, gx, per, rx, 128), BF16),
-            pltpu.VMEM((GROUPS, per, rx, 128), BF16),
-            pltpu.VMEM((GROUPS, per, rx, 128), BF16),
-            pltpu.VMEM((GROUPS, per, rx, 128), BF16),
-            pltpu.VMEM((GROUPS, 2, per // 2, rx, 128), BF16),
-            pltpu.VMEM((GROUPS, 2, per, rx, 128), BF16),
-            pltpu.VMEM((GROUPS, gy, per // 8, 8 * ni, 128), BF16),
-            pltpu.VMEM((GROUPS, gy - 1, per // 8, 8 * ni, 128), BF16),
-            dma((GROUPS,)), dma((GROUPS,)),
-            dma((GROUPS, 6)), dma((GROUPS, 6)),
-            dma((GROUPS, gy - 1)), dma((GROUPS, gy - 1)),
-        ],
-        compiler_params=pltpu.CompilerParams(collective_id=1, has_side_effects=True),
-        name="reduce",
-    )(rows, ut, dz).reshape(ni, 1, nt, 128)
+    )(rows, tile_rows, feed, tall, seeds).reshape(ni, 1, nt, 128)
 
 
 def solution(mesh, gx=GRID_X, gy=GRID_Y):

time: 184 us -> 172 us (0.935)
  Pallas kernels: 182 us -> 170 us
    pallas_call x1 -> x0, Pallas kernels: 34.7 us -> none  [local(): pl.pallas_call(functools.partial(reduce_kernel, gx, gy, nb, nmb), out_sha...]
    pallas_call x1, Pallas kernels: 148 us -> 170 us  [local(): pl.pallas_call(functools.partial(relay_kernel, sections, nmb, nb, gx, gy)...]
where the time goes in v3:
time: 172 us
  Pallas kernels  170 us (99%)
    pallas_call x1, Pallas kernels, local(): pl.pallas_call(functools.partial(relay_kernel, sections, nmb, nb, gx, gy)...  170 us

profile of v3, /device:TPU:6, one launch (start us, length us, event | category | flops | bytes accessed | tf_op | source)
XLA Modules:
  0.0 171.6 jit_solution(5660759915427345470)
XLA Ops:
  0.0 170.0 %relay.1 = f32[2,72,128]{2,1,0:T(8,128)} custom-call(s32[72]{0:T(128)} %bitcast.15, s32[1,72]{1,0:T(1,128)} %line_ref.1, bf16[16,24,8,128]{3,2,1,0:T(8,128)(2,1)} %bitcast.12, bf16[24,384,128]{2,1,0:T(8,128)(2,1)} %bitcast.11, bf16[16,24,8,128]{3,2,1,0:T(8,128)(2,1)} %bitcast.13), custom_call_target="tpu_custom_call" | custom-call | tf_op jit(solution)/shard_map/relay/pallas_call | solution.py:445
  170.0 1.5 copy.7

commit v4 on v3

--- a/solution.py
+++ b/solution.py
@@ -12,6 +12,7 @@
 CHUNKS = 2
 CHAINS = 2
 AHEAD = 6
+LAG = 4
 GRID_X = 4
 GRID_Y = 8
 GROUPS = 3
@@ -36,22 +37,15 @@
 
 def relay_kernel(sections, nmb, nb, gx, gy, rows_ref, line_ref, x_ref, t_ref, og_ref,
                  out_ref,
-                 dzo, dzg, uto, uts, utg, own, so, sr, sl, ro, got1, sy, got2,
+                 dzb, ub, uts, own, so, sr, sl, ro, got1, sy, got2,
                  hbuf, gbuf, fout, gout, hw, act, scl, prod, pref, flip, board, table, tsem,
-                 fsend, frecv, bsend, brecv, dsend, drecv, us, ur, s1, r1, s2, r2):
+                 fsend, frecv, bsend, brecv, dsend, drecv, us, ur, s1, r1, s2, r2, xsend, xrecv, ready):
     sec = lax.axis_index("section")
+    dp = lax.axis_index("dp")
     nt = 3 * nb
     width = nb * 128
     per = nb // CHUNKS
     run = nt // CHAINS
-    first = sec == 0
-    final = sec == sections - 1
-    dp = lax.axis_index("dp")
-    swap = dp + 1 - 2 * lax.rem(dp, 2)
-    straight = sections - 1 - lax.rem(sections - 1, 2)
-    up = {"dp": jnp.where(sec < straight, swap, dp), "section": jnp.minimum(sec + 1, sections - 1)}
-    down = {"dp": jnp.where(sec - 1 < straight, swap, dp), "section": jnp.maximum(sec - 1, 0)}
-
     ni = 128 // (2 * gx * gy)
     rx = gy * ni
     tper = nt // GROUPS
@@ -60,6 +54,21 @@
     me_c = lax.rem(dp, 2)
     me_x = lax.rem(dp // 2, gx)
     me_y = dp // (2 * gx)
+    first = sec == 0
+    final = sec == sections - 1
+    odd = me_c == 1
+    worker = first & odd
+    idle = first & jnp.logical_not(odd)
+    feeder = (sec == 1) & jnp.logical_not(odd)
+    swap = dp + 1 - 2 * me_c
+    straight = sections - 1 - lax.rem(sections - 1, 2)
+    above = jnp.minimum(sec + 1, sections - 1)
+    below = jnp.maximum(sec - 1, 0)
+    up_dp = jnp.where(sec < straight, swap, dp)
+    down_dp = jnp.where(sec == 1, dp + 1 - me_c, jnp.where(sec - 1 < straight, swap, dp))
+    offset = jnp.where((sec == 1) & odd, nmb, 0)
+    down = {"dp": down_dp, "section": below}
+    mate = {"dp": swap}
 
     def at(y, x):
         return {"dp": (y * gx + x) * 2 + me_c}
@@ -67,67 +76,120 @@
     x_right = lax.rem(me_x + 1, gx)
     x_left = lax.rem(me_x + gx - 1, gx)
     x_over = lax.rem(me_x + 2, gx)
-    mate = {"dp": swap}
     right = at(me_y, x_right)
     left = at(me_y, x_left)
     ys = [at(lax.rem(me_y + j, gy), me_x) for j in range(1, gy)]
 
     barrier = pltpu.get_barrier_semaphore()
 
+    def greet(peer):
+        pl.semaphore_signal(barrier, inc=1, device_id=peer, device_id_type=MESH)
+
     @pl.when(sec > 0)
     def _():
-        pl.semaphore_signal(barrier, inc=1, device_id=down, device_id_type=MESH)
-
-    @pl.when(sec < sections - 1)
-    def _():
-        pl.semaphore_signal(barrier, inc=1, device_id=up, device_id_type=MESH)
-
-    for peer in ys + [left, right, mate]:
-        pl.semaphore_signal(barrier, inc=1, device_id=peer, device_id_type=MESH)
-
-    pl.semaphore_wait(barrier, gy + 2 + jnp.where(first, 0, 1) + jnp.where(final, 0, 1))
-
-    def fcopy(k, j):
-        return pltpu.make_async_remote_copy(
-            src_ref=fout.at[k, pl.ds(j * per, per)],
-            dst_ref=hbuf.at[k, pl.ds(j * per, per)],
-            send_sem=fsend.at[k],
-            recv_sem=frecv.at[k],
-            device_id=up,
+        greet(down)
+
+    @pl.when((sec > 0) & (sec < sections - 1))
+    def _():
+        greet({"dp": up_dp, "section": above})
+
+    @pl.when(worker)
+    def _():
+        greet({"dp": swap, "section": above})
+        greet({"dp": dp, "section": above})
+
+    for peer in [left, right] + ys:
+        greet(peer)
+
+    @pl.when(jnp.logical_not(idle))
+    def _():
+        greet(mate)
+
+    count = gy + 1 + jnp.where(first, jnp.where(odd, 2, 1), 2 + jnp.where(final, 0, 1))
+    pl.semaphore_wait(barrier, count)
+
+    @pl.when(idle)
+    def _():
+        pl.semaphore_signal(ready, inc=1, device_id=mate, device_id_type=MESH)
+
+    def xcopy(k):
+        return pltpu.make_async_remote_copy(
+            src_ref=x_ref.at[k], dst_ref=hbuf.at[nmb + k], send_sem=xsend.at[k], recv_sem=xrecv.at[k],
+            device_id={"dp": dp + 1 - me_c, "section": below}, device_id_type=MESH,
+        )
+
+    @pl.when(feeder)
+    def _():
+        def feed(k, carry):
+            xcopy(k).start()
+            return carry
+
+        lax.fori_loop(0, nmb, feed, 0)
+
+    def target(slot):
+        return {"dp": jnp.where(first & (slot >= nmb), dp, up_dp), "section": above}
+
+    def fcopy(slot, j):
+        return pltpu.make_async_remote_copy(
+            src_ref=fout.at[slot, pl.ds(j * per, per)],
+            dst_ref=hbuf.at[lax.rem(slot, nmb), pl.ds(j * per, per)],
+            send_sem=fsend.at[slot],
+            recv_sem=frecv.at[lax.rem(slot, nmb)],
+            device_id=target(slot),
             device_id_type=MESH,
         )
 
     def bcopy(k, j):
         return pltpu.make_async_remote_copy(
             src_ref=gout.at[k, pl.ds(j * per, per)],
-            dst_ref=gbuf.at[k, pl.ds(j * per, per)],
+            dst_ref=gbuf.at[k + offset, pl.ds(j * per, per)],
             send_sem=bsend.at[k],
-            recv_sem=brecv.at[k],
+            recv_sem=brecv.at[k + offset],
             device_id=down,
             device_id_type=MESH,
         )
 
-    def fwhole(k):
-        return pltpu.make_async_remote_copy(
+    def fsent(slot):
+        pltpu.make_async_remote_copy(
+            src_ref=fout.at[slot], dst_ref=hbuf.at[lax.rem(slot, nmb)], send_sem=fsend.at[slot],
+            recv_sem=frecv.at[lax.rem(slot, nmb)], device_id=target(slot), device_id_type=MESH,
+        ).wait_send()
+
+    def fgot(k):
+        pltpu.make_async_remote_copy(
             src_ref=fout.at[k], dst_ref=hbuf.at[k], send_sem=fsend.at[k], recv_sem=frecv.at[k],
-            device_id=up, device_id_type=MESH,
-        )
-
-    def bwhole(k):
-        return pltpu.make_async_remote_copy(
-            src_ref=gout.at[k], dst_ref=gbuf.at[k], send_sem=bsend.at[k], recv_sem=brecv.at[k],
+            device_id=target(k), device_id_type=MESH,
+        ).wait_recv()
+
+    def bsent(k):
+        pltpu.make_async_remote_copy(
+            src_ref=gout.at[k], dst_ref=gbuf.at[k + offset], send_sem=bsend.at[k], recv_sem=brecv.at[k + offset],
             device_id=down, device_id_type=MESH,
-        )
-
-    def dcopy(k):
-        return pltpu.make_async_remote_copy(
-            src_ref=dzo.at[k], dst_ref=dzg.at[k], send_sem=dsend.at[k], recv_sem=drecv.at[k],
+        ).wait_send()
+
+    def bgot(slot):
+        pltpu.make_async_remote_copy(
+            src_ref=gout.at[lax.rem(slot, nmb)], dst_ref=gbuf.at[slot], send_sem=bsend.at[lax.rem(slot, nmb)],
+            recv_sem=brecv.at[slot], device_id=down, device_id_type=MESH,
+        ).wait_recv()
+
+    def dcopy(slot):
+        place = lax.rem(slot + nmb, 2 * nmb)
+        return pltpu.make_async_remote_copy(
+            src_ref=dzb.at[slot], dst_ref=dzb.at[place], send_sem=dsend.at[slot], recv_sem=drecv.at[place],
             device_id=mate, device_id_type=MESH,
         )
 
-    def ucopy():
-        return pltpu.make_async_remote_copy(
-            src_ref=uts, dst_ref=utg, send_sem=us, recv_sem=ur, device_id=mate, device_id_type=MESH,
+    def dgot(slot):
+        pltpu.make_async_remote_copy(
+            src_ref=dzb.at[slot], dst_ref=dzb.at[slot], send_sem=dsend.at[slot], recv_sem=drecv.at[slot],
+            device_id=mate, device_id_type=MESH,
+        ).wait_recv()
+
+    def ucopy(h):
+        return pltpu.make_async_remote_copy(
+            src_ref=uts.at[h], dst_ref=ub.at[1 - h], send_sem=us.at[h], recv_sem=ur.at[1 - h],
+            device_id=mate, device_id_type=MESH,
         )
 
     def setup():
@@ -164,29 +226,33 @@
         lax.fori_loop(0, nb, turn, 0)
         copy.wait()
 
-    def turned():
+    def turned(h):
         order = arrange(gx, gy)
 
         def one(b, carry):
-            q = hbuf[:, b].astype(F32) * scl[...]
+            q = hbuf[h * nmb:(h + 1) * nmb, b].astype(F32) * scl[h * nmb:(h + 1) * nmb]
             u = q.reshape(nmb * MB, 128).astype(BF16)
             moved = lax.dot_general(order, u, (((1,), (1,)), ((), ())), preferred_element_type=F32)
             moved = moved.astype(BF16)
-            uto[b] = moved[:64]
-            uts[b] = moved[64:]
+            ub[h, b] = moved[:64]
+            uts[h, b] = moved[64:]
             return carry
 
         lax.fori_loop(0, nb, one, 0)
-        ucopy().start()
+        ucopy(h).start()
 
     def forward(k, carry):
-        @pl.when(first)
+        @pl.when(first & (k < nmb))
         def _():
-            hbuf[k] = x_ref[k]
+            hbuf[k] = x_ref[lax.rem(k, nmb)]
+
+        @pl.when(first & (k >= nmb))
+        def _():
+            xcopy(k - nmb).wait_recv()
 
         @pl.when(sec > 0)
         def _():
-            fwhole(k).wait_recv()
+            fgot(k)
 
         total = jnp.zeros((MB, 128), F32)
         for b in range(nb):
@@ -210,9 +276,9 @@
         return carry
 
     def ending(k, carry):
-        bwhole(k).wait_recv()
+        bgot(k)
         for c in range(nb):
-            dzo[k, c] = (gbuf[k, c].astype(F32) * act[k, c]).astype(BF16)
+            dzb[k, c] = (gbuf[k, c].astype(F32) * act[k, c]).astype(BF16)
         dcopy(k).start()
         return carry
 
@@ -223,11 +289,11 @@
 
         @pl.when(sec < sections - 1)
         def _():
-            bwhole(k).wait_recv()
+            bgot(k)
 
         for c in range(nb):
             dz = (gbuf[k, c].astype(F32) * act[k, c]).astype(BF16)
-            dzo[k, c] = dz
+            dzb[k, c] = dz
             back = jnp.dot(dz, flip[c], preferred_element_type=F32)
             for i in range(3):
                 prod[3 * c + i] = back[:, i * 128:(i + 1) * 128]
@@ -258,45 +324,69 @@
         return carry
 
     early = sec >= sections // 2
+    late = jnp.logical_not(early | first)
     warm = jnp.minimum(1 + AHEAD * (sections - 1 - sec), nmb)
+    rounds = jnp.where(first, jnp.where(odd, 2 * nmb, 0), warm)
+    paired = jnp.where(first, 0, nmb - warm)
 
     @pl.when(early)
     def _():
         setup()
 
-    lax.fori_loop(0, warm, forward, 0)
-
-    @pl.when(jnp.logical_not(early))
+    def opening(i, carry):
+        j = i - LAG
+        mixed = jnp.where(lax.rem(j, 2) == 0, nmb + j // 2, LAG + j // 2)
+        mixed = jnp.where(i < LAG, i, jnp.where(i >= 2 * nmb - LAG, i, mixed))
+        return forward(jnp.where(first, mixed, i), carry)
+
+    lax.fori_loop(0, rounds, opening, 0)
+
+    @pl.when(late)
     def _():
         setup()
-        turned()
+        turned(0)
+
+    @pl.when(worker)
+    def _():
+        pl.semaphore_wait(ready, 1)
+        turned(0)
+        turned(1)
 
     def both(k, carry):
         backward(k, carry)
         forward(k + warm, carry)
         return carry
 
-    lax.fori_loop(0, nmb - warm, both, 0)
+    lax.fori_loop(0, paired, both, 0)
 
     @pl.when(sec > 0)
     def _():
         lax.fori_loop(nmb - warm, nmb, backward, 0)
 
-    @pl.when(first)
-    def _():
-        lax.fori_loop(0, nmb, ending, 0)
+    @pl.when(worker)
+    def _():
+        def alternate(i, carry):
+            return ending(i // 2 + nmb * lax.rem(i, 2), carry)
+
+        lax.fori_loop(0, 2 * nmb, alternate, 0)
 
     @pl.when(early)
     def _():
-        turned()
-
-    ucopy().wait_recv()
+        turned(0)
+
+    @pl.when(idle)
+    def _():
+        ucopy(1).wait_recv()
+
+    @pl.when(jnp.logical_not(worker))
+    def _():
+        ucopy(0).wait_recv()
 
     def arrived(k, carry):
-        dcopy(k).wait_recv()
-        return carry
-
-    lax.fori_loop(0, nmb, arrived, 0)
+        dgot(k)
+        return carry
+
+    lax.fori_loop(jnp.where(first, jnp.where(odd, 2 * nmb, 0), nmb), 2 * nmb, arrived, 0)
 
     low, high = pl.ds(0, half), pl.ds(half, half)
 
@@ -324,12 +414,10 @@
     for g in range(GROUPS):
         def column(c, carry, g=g):
             col = g * (tper // 3) + c
-            mine = dzo[:, col].astype(F32).reshape(nmb * MB, 128)
-            theirs = dzg[:, col].astype(F32).reshape(nmb * MB, 128)
-            d = jnp.concatenate([mine, theirs], axis=0).astype(BF16)
+            d = dzb[:, col].astype(F32).reshape(2 * nmb * MB, 128).astype(BF16)
             for i in range(3):
                 row = rows_ref[3 * col + i]
-                wide = jnp.concatenate([uto[row], utg[row]], axis=1)
+                wide = jnp.concatenate([ub[0, row], ub[1, row]], axis=1)
                 full = jnp.dot(wide, d, preferred_element_type=F32)
                 for x in range(gx):
                     own[g, x, 3 * c + i] = full[x * rx:(x + 1) * rx]
@@ -407,21 +495,36 @@
             copy1(g, kind).wait_send()
         for j in range(1, gy):
             copy2(g, j).wait_send()
-    ucopy().wait_send()
-
-    def drain(k, carry):
-        @pl.when(sec < sections - 1)
-        def _():
-            fwhole(k).wait_send()
-
-        @pl.when(sec > 0)
-        def _():
-            bwhole(k).wait_send()
-
+
+    @pl.when(jnp.logical_not(idle))
+    def _():
+        ucopy(0).wait_send()
+
+    @pl.when(worker)
+    def _():
+        ucopy(1).wait_send()
+
+    def fdrain(k, carry):
+        fsent(k)
+        return carry
+
+    def bdrain(k, carry):
+        bsent(k)
+        return carry
+
+    def ddrain(k, carry):
         dcopy(k).wait_send()
         return carry
 
-    lax.fori_loop(0, nmb, drain, 0)
+    def xdrain(k, carry):
+        xcopy(k).wait_send()
+        return carry
+
+    sent = jnp.where(first, jnp.where(odd, 2 * nmb, 0), nmb)
+    lax.fori_loop(0, jnp.where(final, 0, sent), fdrain, 0)
+    lax.fori_loop(0, jnp.where(first, 0, nmb), bdrain, 0)
+    lax.fori_loop(0, sent, ddrain, 0)
+    lax.fori_loop(0, jnp.where(feeder, nmb, 0), xdrain, 0)
 
 
 def local(gx, gy, inputs, tiles, tile_rows, out_grad):
@@ -441,15 +544,16 @@
     ni = 128 // (2 * gx * gy)
     rx = gy * ni
     tper = nt // GROUPS
-    strip = (nb, 64, nmb * MB)
+    strip = (2, nb, 64, nmb * MB)
+    twice = (2 * nmb, nb, MB, 128)
     return pl.pallas_call(
         functools.partial(relay_kernel, sections, nmb, nb, gx, gy),
         out_shape=jax.ShapeDtypeStruct((ni, nt, 128), F32),
         in_specs=[smem] + [vmem] * 4,
         out_specs=vmem,
         scratch_shapes=[
-            pltpu.VMEM(piece, BF16), pltpu.VMEM(piece, BF16),
-            pltpu.VMEM(strip, BF16), pltpu.VMEM(strip, BF16), pltpu.VMEM(strip, BF16),
+            pltpu.VMEM(twice, BF16),
+            pltpu.VMEM(strip, BF16), pltpu.VMEM(strip, BF16),
             pltpu.VMEM((GROUPS, gx, tper, rx, 128), F32),
             pltpu.VMEM((GROUPS, tper, rx, 128), BF16),
             pltpu.VMEM((GROUPS, tper, rx, 128), BF16),
@@ -458,20 +562,21 @@
             pltpu.VMEM((GROUPS, 2, tper, rx, 128), BF16),
             pltpu.VMEM((GROUPS, gy, tper // 8, 8 * ni, 128), BF16),
             pltpu.VMEM((GROUPS, gy - 1, tper // 8, 8 * ni, 128), BF16),
-            pltpu.VMEM(piece, BF16), pltpu.VMEM(piece, BF16), pltpu.VMEM(piece, BF16), pltpu.VMEM(piece, BF16),
+            pltpu.VMEM(twice, BF16), pltpu.VMEM(twice, BF16), pltpu.VMEM(twice, BF16), pltpu.VMEM(piece, BF16),
             pltpu.VMEM((nb, MB, 128), BF16),
-            pltpu.VMEM(piece, F32),
-            pltpu.VMEM((nmb, MB, 128), F32),
+            pltpu.VMEM(twice, F32),
+            pltpu.VMEM((2 * nmb, MB, 128), F32),
             pltpu.VMEM((nt, MB, 128), F32),
             pltpu.VMEM((nt, MB, 128), F32),
             pltpu.VMEM((nb, 128, 3 * 128), BF16),
             pltpu.VMEM((8, 128), jnp.int32),
             pltpu.SMEM((8, 128), jnp.int32),
             dma(()),
-            dma((nmb,)), dma((nmb,)), dma((nmb,)), dma((nmb,)), dma((nmb,)), dma((nmb,)),
-            dma(()), dma(()),
+            dma((2 * nmb,)), dma((nmb,)), dma((nmb,)), dma((2 * nmb,)), dma((2 * nmb,)), dma((2 * nmb,)),
+            dma((2,)), dma((2,)),
             dma((GROUPS, 6)), dma((GROUPS, 6)),
             dma((GROUPS, gy - 1)), dma((GROUPS, gy - 1)),
+            dma((nmb,)), dma((nmb,)), pltpu.SemaphoreType.REGULAR,
         ],
         compiler_params=pltpu.CompilerParams(collective_id=0, has_side_effects=True),
         name="relay",

time: 172 us -> 167 us (0.971)
  Pallas kernels: 170 us -> 165 us
    pallas_call x1, Pallas kernels: 170 us -> 165 us  [local(): pl.pallas_call(functools.partial(relay_kernel, sections, nmb, nb, gx, gy)...]
where the time goes in v4:
time: 167 us
  Pallas kernels  165 us (99%)
    pallas_call x1, Pallas kernels, local(): pl.pallas_call(functools.partial(relay_kernel, sections, nmb, nb, gx, gy)...  165 us

profile of v4, /device:TPU:6, one launch (start us, length us, event | category | flops | bytes accessed | tf_op | source)
XLA Modules:
  0.0 166.8 jit_solution(8450394422285665475)
XLA Ops:
  0.0 165.2 %relay.1 = f32[2,72,128]{2,1,0:T(8,128)} custom-call(s32[72]{0:T(128)} %bitcast.15, s32[1,72]{1,0:T(1,128)} %line_ref.1, bf16[16,24,8,128]{3,2,1,0:T(8,128)(2,1)} %bitcast.12, bf16[24,384,128]{2,1,0:T(8,128)(2,1)} %bitcast.11, bf16[16,24,8,128]{3,2,1,0:T(8,128)(2,1)} %bitcast.13), custom_call_target="tpu_custom_call" | custom-call | tf_op jit(solution)/shard_map/relay/pallas_call | solution.py:549
  165.2 1.5 copy.7

commit v5 on v4

--- a/solution.py
+++ b/solution.py
@@ -12,7 +12,7 @@
 CHUNKS = 2
 CHAINS = 2
 AHEAD = 6
-LAG = 4
+LAG = 2
 GRID_X = 4
 GRID_Y = 8
 GROUPS = 3
@@ -39,7 +39,7 @@
                  out_ref,
                  dzb, ub, uts, own, so, sr, sl, ro, got1, sy, got2,
                  hbuf, gbuf, fout, gout, hw, act, scl, prod, pref, flip, board, table, tsem,
-                 fsend, frecv, bsend, brecv, dsend, drecv, us, ur, s1, r1, s2, r2, xsend, xrecv, ready):
+                 fsend, frecv, bsend, brecv, dsend, drecv, us, ur, s1, r1, s2, r2, xsend, xrecv, ready, go):
     sec = lax.axis_index("section")
     dp = lax.axis_index("dp")
     nt = 3 * nb
@@ -99,18 +99,11 @@
         greet({"dp": dp, "section": above})
 
     for peer in [left, right] + ys:
-        greet(peer)
+        greet({"dp": jnp.where(first, peer["dp"] - me_c, peer["dp"])})
 
     @pl.when(jnp.logical_not(idle))
     def _():
         greet(mate)
-
-    count = gy + 1 + jnp.where(first, jnp.where(odd, 2, 1), 2 + jnp.where(final, 0, 1))
-    pl.semaphore_wait(barrier, count)
-
-    @pl.when(idle)
-    def _():
-        pl.semaphore_signal(ready, inc=1, device_id=mate, device_id_type=MESH)
 
     def xcopy(k):
         return pltpu.make_async_remote_copy(
@@ -118,13 +111,29 @@
             device_id={"dp": dp + 1 - me_c, "section": below}, device_id_type=MESH,
         )
 
+    @pl.when(worker)
+    def _():
+        pl.semaphore_wait(barrier, 2)
+        pl.semaphore_signal(go, inc=1, device_id={"dp": swap, "section": above}, device_id_type=MESH)
+
     @pl.when(feeder)
     def _():
+        pl.semaphore_wait(go, 1)
+
         def feed(k, carry):
             xcopy(k).start()
             return carry
 
         lax.fori_loop(0, nmb, feed, 0)
+
+    @pl.when(jnp.logical_not(worker))
+    def _():
+        plane = gy + 2 + jnp.where(first, gy + 1, 1 + jnp.where(final, 0, 1))
+        pl.semaphore_wait(barrier, plane)
+
+    @pl.when(idle)
+    def _():
+        pl.semaphore_signal(ready, inc=1, device_id=mate, device_id_type=MESH)
 
     def target(slot):
         return {"dp": jnp.where(first & (slot >= nmb), dp, up_dp), "section": above}
@@ -576,7 +585,7 @@
             dma((2,)), dma((2,)),
             dma((GROUPS, 6)), dma((GROUPS, 6)),
             dma((GROUPS, gy - 1)), dma((GROUPS, gy - 1)),
-            dma((nmb,)), dma((nmb,)), pltpu.SemaphoreType.REGULAR,
+            dma((nmb,)), dma((nmb,)), pltpu.SemaphoreType.REGULAR, pltpu.SemaphoreType.REGULAR,
         ],
         compiler_params=pltpu.CompilerParams(collective_id=0, has_side_effects=True),
         name="relay",

time: 167 us -> 168 us (level)
  no operation moved by 1% of the time
where the time goes in v5:
time: 168 us; the launch traced here: 167 us
  Pallas kernels  165 us (98%)
    pallas_call x1, Pallas kernels, local(): pl.pallas_call(functools.partial(relay_kernel, sections, nmb, nb, gx, gy)...  165 us

profile of v5, /device:TPU:6, one launch (start us, length us, event | category | flops | bytes accessed | tf_op | source)
XLA Modules:
  0.0 166.7 jit_solution(8428089711197906883)
XLA Ops:
  0.0 165.1 %relay.1 = f32[2,72,128]{2,1,0:T(8,128)} custom-call(s32[72]{0:T(128)} %bitcast.15, s32[1,72]{1,0:T(1,128)} %line_ref.1, bf16[16,24,8,128]{3,2,1,0:T(8,128)(2,1)} %bitcast.12, bf16[24,384,128]{2,1,0:T(8,128)(2,1)} %bitcast.11, bf16[16,24,8,128]{3,2,1,0:T(8,128)(2,1)} %bitcast.13), custom_call_target="tpu_custom_call" | custom-call | tf_op jit(solution)/shard_map/relay/pallas_call | solution.py:558
  165.1 1.5 copy.7

commit v6 on v4

--- a/solution.py
+++ b/solution.py
@@ -38,7 +38,7 @@
 def relay_kernel(sections, nmb, nb, gx, gy, rows_ref, line_ref, x_ref, t_ref, og_ref,
                  out_ref,
                  dzb, ub, uts, own, so, sr, sl, ro, got1, sy, got2,
-                 hbuf, gbuf, fout, gout, hw, act, scl, prod, pref, flip, board, table, tsem,
+                 hbuf, gbuf, fout, gout, hw, duo, act, scl, prod, pref, flip, board, table, tsem,
                  fsend, frecv, bsend, brecv, dsend, drecv, us, ur, s1, r1, s2, r2, xsend, xrecv, ready):
     sec = lax.axis_index("section")
     dp = lax.axis_index("dp")
@@ -220,10 +220,11 @@
 
         def turn(c, carry):
             for i in range(3):
-                flip[c, :, i * 128:(i + 1) * 128] = t_ref[c, i * 128:(i + 1) * 128, :].T
-            return carry
-
-        lax.fori_loop(0, nb, turn, 0)
+                for e in range(2):
+                    flip[c, e * 128:(e + 1) * 128, i * 128:(i + 1) * 128] = t_ref[2 * c + e, i * 128:(i + 1) * 128, :].T
+            return carry
+
+        lax.fori_loop(0, nb // 2, turn, 0)
         copy.wait()
 
     def turned(h):
@@ -259,13 +260,18 @@
             h = hbuf[k, b]
             hf = h.astype(F32)
             total = total + hf * hf
-            hw[b] = h
+            hw[b] = hf
         mean = jnp.sum(total, axis=1, keepdims=True) * (1.0 / width)
         scale = jnp.broadcast_to(lax.rsqrt(mean + EPS), (MB, 128))
         scl[k] = scale
         for c in range(nb):
-            left = jnp.concatenate([hw[rows_ref[3 * c + i]] for i in range(3)], axis=1)
-            z = jnp.dot(left, t_ref[c], preferred_element_type=F32)
+            if c % 2 == 0:
+                left = jnp.concatenate(
+                    [jnp.concatenate([hw[rows_ref[3 * c + i]], hw[rows_ref[3 * c + 3 + i]]], axis=0) for i in range(3)],
+                    axis=1,
+                ).astype(BF16)
+                wide = jnp.dot(left, duo[c // 2], preferred_element_type=F32)
+            z = wide[(c % 2) * MB:(c % 2 + 1) * MB, (c % 2) * 128:(c % 2 + 1) * 128]
             a = jnp.tanh(z * scale)
             act[k, c] = 1.0 - a * a
             fout[k, c] = (hbuf[k, c].astype(F32) + a).astype(BF16)
@@ -291,12 +297,20 @@
         def _():
             bgot(k)
 
-        for c in range(nb):
-            dz = (gbuf[k, c].astype(F32) * act[k, c]).astype(BF16)
-            dzb[k, c] = dz
-            back = jnp.dot(dz, flip[c], preferred_element_type=F32)
+        blank = jnp.zeros((MB, 128), F32)
+        for c in range(0, nb, 2):
+            both_dz = []
+            for e in range(2):
+                dz = (gbuf[k, c + e].astype(F32) * act[k, c + e]).astype(BF16)
+                dzb[k, c + e] = dz
+                both_dz.append(dz.astype(F32))
+            upper = jnp.concatenate([both_dz[0], blank], axis=0)
+            lower = jnp.concatenate([blank, both_dz[1]], axis=0)
+            wide = jnp.concatenate([upper, lower], axis=1).astype(BF16)
+            back = jnp.dot(wide, flip[c // 2], preferred_element_type=F32)
             for i in range(3):
-                prod[3 * c + i] = back[:, i * 128:(i + 1) * 128]
+                prod[3 * c + i] = back[:MB, i * 128:(i + 1) * 128]
+                prod[3 * c + 3 + i] = back[MB:, i * 128:(i + 1) * 128]
         scale = scl[k]
         for j in range(CHAINS):
             acc = prod[table[0, run * j]]
@@ -323,6 +337,12 @@
         dcopy(k).start()
         return carry
 
+    def pair(c, carry):
+        duo[c, :, :128] = t_ref[2 * c]
+        duo[c, :, 128:] = t_ref[2 * c + 1]
+        return carry
+
+    lax.fori_loop(0, nb // 2, pair, 0)
     early = sec >= sections // 2
     late = jnp.logical_not(early | first)
     warm = jnp.minimum(1 + AHEAD * (sections - 1 - sec), nmb)
@@ -563,12 +583,13 @@
             pltpu.VMEM((GROUPS, gy, tper // 8, 8 * ni, 128), BF16),
             pltpu.VMEM((GROUPS, gy - 1, tper // 8, 8 * ni, 128), BF16),
             pltpu.VMEM(twice, BF16), pltpu.VMEM(twice, BF16), pltpu.VMEM(twice, BF16), pltpu.VMEM(piece, BF16),
-            pltpu.VMEM((nb, MB, 128), BF16),
+            pltpu.VMEM((nb, MB, 128), F32),
+            pltpu.VMEM((nb // 2, 3 * 128, 256), BF16),
             pltpu.VMEM(twice, F32),
             pltpu.VMEM((2 * nmb, MB, 128), F32),
             pltpu.VMEM((nt, MB, 128), F32),
             pltpu.VMEM((nt, MB, 128), F32),
-            pltpu.VMEM((nb, 128, 3 * 128), BF16),
+            pltpu.VMEM((nb // 2, 256, 3 * 128), BF16),
             pltpu.VMEM((8, 128), jnp.int32),
             pltpu.SMEM((8, 128), jnp.int32),
             dma(()),

time: 167 us -> 162 us (0.970)
  Pallas kernels: 165 us -> 159 us
    pallas_call x1, Pallas kernels: 165 us -> 159 us  [local(): pl.pallas_call(functools.partial(relay_kernel, sections, nmb, nb, gx, gy)...]
where the time goes in v6:
time: 162 us; the launch traced here: 161 us
  Pallas kernels  159 us (98%)
    pallas_call x1, Pallas kernels, local(): pl.pallas_call(functools.partial(relay_kernel, sections, nmb, nb, gx, gy)...  159 us

profile of v6, /device:TPU:6, one launch (start us, length us, event | category | flops | bytes accessed | tf_op | source)
XLA Modules:
  0.0 161.0 jit_solution(10918746939840777439)
XLA Ops:
  0.0 159.4 %relay.1 = f32[2,72,128]{2,1,0:T(8,128)} custom-call(s32[72]{0:T(128)} %bitcast.15, s32[1,72]{1,0:T(1,128)} %line_ref.1, bf16[16,24,8,128]{3,2,1,0:T(8,128)(2,1)} %bitcast.12, bf16[24,384,128]{2,1,0:T(8,128)(2,1)} %bitcast.11, bf16[16,24,8,128]{3,2,1,0:T(8,128)(2,1)} %bitcast.13), custom_call_target="tpu_custom_call" | custom-call | tf_op jit(solution)/shard_map/relay/pallas_call | solution.py:569
  159.5 1.5 copy.7

commit v7 on v6

--- a/solution.py
+++ b/solution.py
@@ -15,7 +15,7 @@
 LAG = 4
 GRID_X = 4
 GRID_Y = 8
-GROUPS = 3
+GROUPS = 9
 MESH = pl.DeviceIdType.MESH
 F32 = jnp.float32
 BF16 = jnp.bfloat16
@@ -433,17 +433,19 @@
 
     for g in range(GROUPS):
         def column(c, carry, g=g):
-            col = g * (tper // 3) + c
+            col = g * tper // 3 + c
             d = dzb[:, col].astype(F32).reshape(2 * nmb * MB, 128).astype(BF16)
             for i in range(3):
-                row = rows_ref[3 * col + i]
+                tile = 3 * col + i
+                row = rows_ref[tile]
                 wide = jnp.concatenate([ub[0, row], ub[1, row]], axis=1)
                 full = jnp.dot(wide, d, preferred_element_type=F32)
                 for x in range(gx):
-                    own[g, x, 3 * c + i] = full[x * rx:(x + 1) * rx]
-            return carry
-
-        lax.fori_loop(0, tper // 3, column, 0)
+                    own[tile // tper, x, lax.rem(tile, tper)] = full[x * rx:(x + 1) * rx]
+            return carry
+
+        if g % 3 == 0:
+            lax.fori_loop(0, tper, column, 0)
 
         def over(t, carry, g=g):
             so[g, t] = own[g, x_over, t].astype(BF16)

time: 162 us -> 163 us (level)
  no operation moved by 1% of the time
where the time goes in v7:
time: 163 us; the launch traced here: 162 us
  Pallas kernels  160 us (98%)
    pallas_call x1, Pallas kernels, local(): pl.pallas_call(functools.partial(relay_kernel, sections, nmb, nb, gx, gy)...  160 us

profile of v7, /device:TPU:6, one launch (start us, length us, event | category | flops | bytes accessed | tf_op | source)
XLA Modules:
  0.0 161.9 jit_solution(9083946265720486755)
XLA Ops:
  0.0 160.3 %relay.1 = f32[2,72,128]{2,1,0:T(8,128)} custom-call(s32[72]{0:T(128)} %bitcast.15, s32[1,72]{1,0:T(1,128)} %line_ref.1, bf16[16,24,8,128]{3,2,1,0:T(8,128)(2,1)} %bitcast.12, bf16[24,384,128]{2,1,0:T(8,128)(2,1)} %bitcast.11, bf16[16,24,8,128]{3,2,1,0:T(8,128)(2,1)} %bitcast.13), custom_call_target="tpu_custom_call" | custom-call | tf_op jit(solution)/shard_map/relay/pallas_call | solution.py:571
  160.3 1.5 copy.7
